TPU v7x, 512 devices: a whole 4x8x8 slice. The times are simulated.
512 devices in a mesh: gx: 32 (over y, x), gy: 16 (over z, core).
Axes of the slice: x: 4, y: 8, z: 8, core: 2. Of those that a mesh axis runs over, the one named last changes fastest.
Arguments:
- spectra: float32 [64, 4, 33, 4, 2048], P('gx', None, None, None, 'gy'), may hold values from 0.05 to 2
- collection: float32 [4, 33, 561], replicated, may hold values from -0.125 to 0.125
- growth_rate: float32 [4, 33], replicated, may hold values from 0.1 to 1
- fall_speed: float32 [4, 33], replicated, may hold values from 0.05 to 0.9
- supersaturation: float32 [64, 4, 2048], P('gx', None, 'gy'), may hold values from -0.4 to 0.4
- courant: float32 [64, 4, 2048], P('gx', None, 'gy'), may hold values from -0.8 to 0.8
- cloudy: int32 [64, 2048], P('gx', 'gy'), may hold values from 0 to 1, as said below
Outputs:
- spectra_out: float32 [64, 4, 33, 4, 2048], P('gx', None, None, None, 'gy')
Inputs may be any that keep to these rules, and one draw needn't show every extreme that they name: A block is the 128 columns of one x-row that lie on one device; each device holds 2 blocks, and a block is cloudy if any of its entries is 1. In every aligned run of 8 devices along gx with one gy index at most 8 blocks are cloudy; in every draw some run has exactly that many, and some device has all 2 of its blocks cloudy.
All inputs are finite; a program needn't handle non-finite values.
Results may differ from a plain program's by a relative error of at most 0.0003.
Values sent between devices are 32-bit elements; how exact they have to be, the bound alone decides.
No kernel may reach another device: no remote copies, remote signals or barrier semaphores. Data moves between devices by JAX's collectives and lax.ppermute only.
A program may use at most 64 MiB of HBM per device.

v0:
```python
import jax
import jax.numpy as jnp
from jax import lax
from jax.experimental import pallas as pl
from jax.experimental.pallas import tpu as pltpu
from jax.sharding import PartitionSpec as P

TYPES = 4
BINS = 33
LEV = 4
BLK = 2
SUB = 2
COLS = 128
ROWS = BLK * TYPES * BINS * LEV
PAIRS = BINS * (BINS + 1) // 2
HALF = 512
TAIL = 64
KDIM = HALF + 2 * TAIL
MROWS = 80
F32 = jnp.float32
BF16 = jnp.bfloat16


def iota(shape, axis):
    return lax.broadcasted_iota(jnp.int32, shape, axis)


def split(x):
    high = x.astype(BF16)
    low = (x - high.astype(F32)).astype(BF16)
    return high, low


def block_row(t, b):
    return (b * TYPES + t) * BINS * LEV


def pair_of_column(col):
    tail = jnp.where(col >= HALF + TAIL, col - TAIL, col)
    first = jnp.where(col < HALF, col & 31, jnp.where(tail < 528, tail - HALF, tail - 528))
    second = jnp.where(
        col < HALF, (first + (col >> 5)) & 31, jnp.where(tail < 528, first + 16, BINS - 1)
    )
    low = jnp.minimum(first, second)
    high = jnp.maximum(first, second)
    pair = low * BINS - ((low * (low - 1)) >> 1) + (high - low)
    return jnp.where(tail > 560, -1, pair)


def edge_kernel(spec, sat, wind, cloudy, coll, growth, fall, edge, lhs, coef, raw, parts):
    lane = iota((1, COLS), 1)
    owner = ((lane + 2) & 127) >> 2
    row8 = iota((8, COLS), 0)
    main = [jnp.zeros((8, COLS), F32) for _ in range(4)]
    last = jnp.zeros((8, COLS), F32)
    for b in range(BLK):
        cloud_row = cloudy[b : b + 1, :].astype(F32)
        for l in range(LEV):
            extra = jnp.where(
                row8 == 1,
                sat[b * LEV + l : b * LEV + l + 1, :],
                jnp.where(row8 == 2, wind[b * LEV + l : b * LEV + l + 1, :], cloud_row),
            )
            for t in range(TYPES):
                spot = (t * BLK + b) * LEV + l
                mine = owner == spot
                start = block_row(t, b) + l
                for q in range(4):
                    piece = spec[pl.ds(start + 32 * q, 8, stride=LEV), :]
                    main[q] = jnp.where(mine, pltpu.roll(piece, 4 * spot, 1), main[q])
                piece = jnp.where(row8 == 0, spec[start + 128 : start + 129, :], extra)
                last = jnp.where(mine, pltpu.roll(piece, 4 * spot, 1), last)
    for q in range(4):
        edge[8 * q : 8 * q + 8, :] = main[q]
    edge[32:40, :] = last

    stacked = jnp.concatenate(
        [
            jnp.concatenate([growth[...], fall[...]], axis=0),
            jnp.zeros((COLS - 2 * TYPES, BINS), F32),
        ],
        axis=0,
    )
    stacked = jnp.concatenate([stacked, jnp.zeros((COLS, COLS - BINS), F32)], axis=1)
    turned = jnp.transpose(stacked)[0:40, :]
    for n in range(2 * TYPES):
        coef[n] = jnp.broadcast_to(turned[:, n : n + 1], (40, COLS))

    raw[...] = jnp.zeros(raw.shape, F32)
    for n in range(KDIM // COLS):
        width = min(COLS, PAIRS - COLS * n)
        for k in range(BINS):
            raw[n, TYPES * k : TYPES * k + TYPES, 0:width] = coll[k, :, COLS * n : COLS * n + width]
    parts[...] = jnp.zeros(parts.shape, BF16)
    for t in range(TYPES):
        for n in range(KDIM // COLS):
            rows = raw[n, pl.ds(t, 40, stride=TYPES), :]
            both = jnp.concatenate(split(rows), axis=0)
            parts[MROWS * t : MROWS * t + MROWS, COLS * n : COLS * n + COLS] = both
    wanted = pair_of_column(iota((1, KDIM), 1))
    chosen = jnp.where(iota((KDIM, KDIM), 0) == wanted, 1.0, 0.0).astype(BF16)
    lhs[...] = jnp.dot(parts[...], chosen, preferred_element_type=F32).astype(BF16)


def condense(main, top, sat, rate_main, rate_top):
    rising = jnp.maximum(sat, 0.0)
    falling = jnp.maximum(-sat, 0.0)
    transfer = rate_main * main
    up = rising * transfer
    down = falling * transfer
    down_top = falling * (rate_top * top)
    arrive_up = jnp.concatenate([jnp.zeros_like(top), up[:-1]], axis=0)
    arrive_down = jnp.concatenate([down[1:], down_top], axis=0)
    new_main = main - up - down + arrive_up + arrive_down
    new_top = top - down_top + up[-1:]
    return new_main, new_top


def store_pairs(main, top, turn, high_ref, low_ref, tail_ref, lanes):
    turn[0:32, :] = main
    turn[32:48, :] = main[0:16]
    for d in range(16):
        other = main if d == 0 else turn[d : d + 32, :]
        high, low = split(main * other)
        high_ref[32 * d : 32 * d + 32, lanes] = high
        low_ref[32 * d : 32 * d + 32, lanes] = low
    square = jnp.where(iota((16, COLS), 0) == 0, top * top, 0.0)
    rest = jnp.concatenate([main[0:16] * main[16:32], main * top, square], axis=0)
    high, low = split(rest)
    tail_ref[0:TAIL, lanes] = high
    tail_ref[TAIL : 2 * TAIL, lanes] = low


def collect(lhs, high_ref, low_ref, tail_ref):
    def part(left, right):
        return jnp.dot(left, right, preferred_element_type=F32)

    return (
        part(lhs[:, 0:HALF], high_ref[...])
        + part(lhs[:, 0:HALF], low_ref[...])
        + part(lhs[:, HALF:KDIM], tail_ref[...])
    )


def main_kernel(spec, sat, cloudy, lhs, coef, settled, turn, high_ref, low_ref, tail_ref):
    def one(n, carry):
        t = n >> 1
        b = n & 1
        start = block_row(t, b)
        left = lhs[pl.ds(pl.multiple_of(t * MROWS, 16), MROWS), :]
        rate = coef[t]
        speed = coef[TYPES + t]
        wet = cloudy[pl.ds(b, 1), :] > 0
        before = []
        state = []
        for l in range(LEV):
            main = spec[pl.ds(start + l, 32, stride=LEV), :]
            top = spec[pl.ds(start + 128 + l, 1), :]
            before.append((main, top))
            row = sat[pl.ds(b * LEV + l, 1), :]
            state.append(condense(main, top, row, rate[0:32], rate[32:33]))
        for step in range(SUB):
            for half in range(2):
                at = 2 * step + half
                for k in range(2):
                    l = 2 * half + k
                    store_pairs(
                        *state[l],
                        turn.at[LEV * step + l],
                        high_ref.at[at],
                        low_ref.at[at],
                        tail_ref.at[at],
                        slice(COLS * k, COLS * k + COLS),
                    )
                gain = collect(left, high_ref.at[at], low_ref.at[at], tail_ref.at[at])
                for k in range(2):
                    l = 2 * half + k
                    mine = gain[:, COLS * k : COLS * k + COLS]
                    main, top = state[l]
                    state[l] = (
                        main + (mine[0:32] + mine[40:72]),
                        top + (mine[32:33] + mine[72:73]),
                    )
        above = None
        for l in reversed(range(LEV)):
            main = jnp.where(wet, state[l][0], before[l][0])
            top = jnp.where(wet, state[l][1], before[l][1])
            over = (jnp.zeros_like(main), jnp.zeros_like(top)) if above is None else above
            settled[n, l, 0:32, :] = main + speed[0:32] * (over[0] - main)
            settled[n, l, 32:33, :] = top + speed[32:33] * (over[1] - top)
            above = (main, top)
        return carry

    lax.fori_loop(0, BLK * TYPES, one, 0)


def finish_kernel(settled, from_left, from_right, wind, lhs, coef, out, turn, high_ref, low_ref, tail_ref):
    lane = iota((1, COLS), 1)
    owner = ((lane + 2) & 127) >> 2
    kind = owner >> 3
    halo = jnp.where((lane & 3) < 2, from_right[...], from_left[...])

    def by_type(pieces):
        value = pieces[0]
        for t in range(1, TYPES):
            value = jnp.where(kind == t, pieces[t], value)
        return value

    rate = by_type([coef[t] for t in range(TYPES)])
    speed = by_type([coef[TYPES + t] for t in range(TYPES)])
    main = halo[0:32]
    top = halo[32:33]
    wet = halo[35:36] > 0
    state = condense(main, top, halo[33:34], rate[0:32], rate[32:33])
    for step in range(SUB):
        store_pairs(
            *state,
            turn.at[step],
            high_ref.at[step],
            low_ref.at[step],
            tail_ref.at[step],
            slice(0, COLS),
        )
        gain = collect(lhs[...], high_ref.at[step], low_ref.at[step], tail_ref.at[step])
        mine = by_type([gain[MROWS * t : MROWS * t + MROWS] for t in range(TYPES)])
        state = (
            state[0] + (mine[0:32] + mine[40:72]),
            state[1] + (mine[32:33] + mine[72:73]),
        )
    highest = (owner & 3) == LEV - 1

    def settle(value, speed):
        above = jnp.where(highest, 0.0, pltpu.roll(value, COLS - 4, 1))
        return value + speed * (above - value)

    edge = jnp.concatenate(
        [
            settle(jnp.where(wet, state[0], main), speed[0:32]),
            settle(jnp.broadcast_to(jnp.where(wet, state[1], top), (8, COLS)), speed[32:40]),
        ],
        axis=0,
    )
    edge_wind = jnp.broadcast_to(halo[34:35], (8, COLS))

    def shifted(value, ghost, by):
        if by > 0:
            return pltpu.roll(jnp.where(lane < by, ghost, value), COLS - by, 1)
        return pltpu.roll(jnp.where(lane >= COLS + by, ghost, value), -by, 1)

    for b in range(BLK):
        for l in range(LEV):
            ghost = pltpu.roll(edge_wind, (COLS - 4 * (b * LEV + l)) % COLS, 1)
            own = jnp.broadcast_to(wind[b * LEV + l : b * LEV + l + 1, :], (8, COLS))
            right = (own + shifted(own, ghost, 1)) * (0.5 / 12.0)
            left = (own + shifted(own, ghost, -1)) * (0.5 / 12.0)
            right_abs = jnp.abs(right)
            left_abs = jnp.abs(left)
            w_p2 = (right + right_abs)[0:1]
            w_p1 = (-(7.0 * right + 3.0 * right_abs) - (left + left_abs))[0:1]
            w_0 = (1.0 - (7.0 * right - 3.0 * right_abs) + (7.0 * left + 3.0 * left_abs))[0:1]
            w_m1 = ((right - right_abs) + (7.0 * left - 3.0 * left_abs))[0:1]
            w_m2 = (left_abs - left)[0:1]
            for t in range(TYPES):
                n = t * BLK + b
                x = settled[n, l]
                g = pltpu.roll(edge, (COLS - 4 * (n * LEV + l)) % COLS, 1)
                y = (
                    w_0 * x
                    + w_p1 * shifted(x, g, 1)
                    + w_m1 * shifted(x, g, -1)
                    + w_p2 * shifted(x, g, 2)
                    + w_m2 * shifted(x, g, -2)
                )
                start = block_row(t, b) + l
                for q in range(4):
                    out[pl.ds(start + 32 * q, 8, stride=LEV), :] = y[8 * q : 8 * q + 8]
                out[start + 128 : start + 129, :] = y[32:33]


def vmem(count):
    return [pl.BlockSpec(memory_space=pltpu.VMEM)] * count


def body(spectra, collection, growth_rate, fall_speed, supersaturation, courant, cloudy):
    spec = spectra.reshape(ROWS, COLS)
    sat = supersaturation.reshape(BLK * LEV, COLS)
    wind = courant.reshape(BLK * LEV, COLS)
    coll = jnp.transpose(collection, (1, 0, 2))
    edge, lhs, coef = pl.pallas_call(
        edge_kernel,
        out_shape=(
            jax.ShapeDtypeStruct((40, COLS), F32),
            jax.ShapeDtypeStruct((TYPES * MROWS, KDIM), BF16),
            jax.ShapeDtypeStruct((2 * TYPES, 40, COLS), F32),
        ),
        in_specs=vmem(7),
        out_specs=tuple(vmem(3)),
        scratch_shapes=[
            pltpu.VMEM((KDIM // COLS, TYPES * 40, COLS), F32),
            pltpu.VMEM((TYPES * MROWS, KDIM), BF16),
        ],
        name="edges",
    )(spec, sat, wind, cloudy, coll, growth_rate, fall_speed)
    count = lax.axis_size("gy")
    up = [(i, (i + 1) % count) for i in range(count)]
    down = [(j, i) for i, j in up]
    from_left = lax.ppermute(edge, "gy", up)
    from_right = lax.ppermute(edge, "gy", down)
    settled = pl.pallas_call(
        main_kernel,
        out_shape=jax.ShapeDtypeStruct((BLK * TYPES, LEV, 40, COLS), F32),
        in_specs=vmem(5),
        out_specs=vmem(1)[0],
        scratch_shapes=[
            pltpu.VMEM((SUB * LEV, 48, COLS), F32),
            pltpu.VMEM((2 * SUB, HALF, 2 * COLS), BF16),
            pltpu.VMEM((2 * SUB, HALF, 2 * COLS), BF16),
            pltpu.VMEM((2 * SUB, 2 * TAIL, 2 * COLS), BF16),
        ],
        name="blocks",
    )(spec, sat, cloudy, lhs, coef)
    out = pl.pallas_call(
        finish_kernel,
        out_shape=jax.ShapeDtypeStruct((ROWS, COLS), F32),
        in_specs=vmem(6),
        out_specs=vmem(1)[0],
        scratch_shapes=[
            pltpu.VMEM((SUB, 48, COLS), F32),
            pltpu.VMEM((SUB, HALF, COLS), BF16),
            pltpu.VMEM((SUB, HALF, COLS), BF16),
            pltpu.VMEM((SUB, 2 * TAIL, COLS), BF16),
        ],
        name="finish",
    )(settled, from_left, from_right, wind, lhs, coef)
    return out.reshape(spectra.shape)


def solution(mesh):
    return jax.shard_map(
        body,
        mesh=mesh,
        in_specs=(
            P("gx", None, None, None, "gy"),
            P(),
            P(),
            P(),
            P("gx", None, "gy"),
            P("gx", None, "gy"),
            P("gx", "gy"),
        ),
        out_specs=P("gx", None, None, None, "gy"),
        check_vma=False,
    )
```

profile of v0, /device:TPU:62, one launch (start us, length us, event | category | flops | bytes accessed | tf_op | source)
XLA Modules:
  0.0 27.7 jit_solution(5061629621464511826)
XLA Ops:
  0.0 2.7 %edges.1 = (f32[40,128]{1,0:T(8,128)}, bf16[320,640]{1,0:T(8,128)(2,1)}, f32[8,40,128]{2,1,0:T(8,128)}) custom-call(f32[1056,128]{1,0:T(8,128)} %bitcast.5, f32[8,128]{1,0:T(8,128)} %bitcast.8, f32[8,128]{1,0:T(8,128)} %bitcast.10, s32[2,128]{1,0:T(2,128)} %cloudy.3, f32[33,4,561]{2,1,0:T(4,128)} %bitcast.7, f32[4,33]{1,0:T(4,128)} %growth.1, f32[4,33]{1,0:T(4,128)} %fall.1), custom_call_target="tpu_custom_call" | custom-call | tf_op jit(solution)/shard_map/edges/pallas_call | solution.py:289
  2.7 8.5 %collective-permute-start.1 = (f32[40,128]{1,0:T(8,128)}, f32[40,128]{1,0:T(8,128)S(1)}, u32[]{:S(2)}, u32[]{:S(2)}) collective-permute-start(f32[40,128]{1,0:T(8,128)} %get-tuple-element.10), channel_id=1, source_target_pairs={{1,0},{2,1},{3,2},{4,3},{5,4},{6,5},{7,6},{8,7},{9,8},{10,9},{11,1... | collective-permute-start | bytes 61448 | tf_op jit(solution)/shard_map/ppermute | solution.py:308
  11.2 0.0 collective-permute-start
  11.2 11.2 %blocks.1.settled = f32[8,4,40,128]{3,2,1,0:T(8,128)} custom-call(f32[1056,128]{1,0:T(8,128)} %bitcast.6, f32[8,128]{1,0:T(8,128)} %bitcast.9, s32[2,128]{1,0:T(2,128)} %cloudy.3, bf16[320,640]{1,0:T(8,128)(2,1)} %get-tuple-element.8.lhs, f32[8,40,128]{2,1,0:T(8,128)} %get-tuple-element.9.coef), custom_call_target="tpu_custom_call" | custom-call | tf_op jit(solution)/shard_map/blocks/pallas_call | solution.py:309
  22.4 0.0 collective-permute-done.1.from_right
  22.4 0.0 copy-start
  22.4 0.0 collective-permute-done.from_left
  22.4 0.6 %copy-done = f32[40,128]{1,0:T(8,128)} copy-done((f32[40,128]{1,0:T(8,128)}, f32[40,128]{1,0:T(8,128)S(1)}, u32[]{:S(2)}) %copy-start) | copy-done | bytes 20504
  23.0 0.0 copy-start.1
  23.0 0.6 %copy-done.1 = f32[40,128]{1,0:T(8,128)} copy-done((f32[40,128]{1,0:T(8,128)}, f32[40,128]{1,0:T(8,128)S(1)}, u32[]{:S(2)}) %copy-start.1) | copy-done | bytes 20504
  23.6 4.1 %finish.1 = f32[1056,128]{1,0:T(8,128)} custom-call(f32[8,4,40,128]{3,2,1,0:T(8,128)} %blocks.1.settled, f32[40,128]{1,0:T(8,128)} %copy-done.1, f32[40,128]{1,0:T(8,128)} %copy-done, f32[8,128]{1,0:T(8,128)} %bitcast.11, bf16[320,640]{1,0:T(8,128)(2,1)} %get-tuple-element.8.lhs, f32[8,40,128]{2,1,0:T(8,128)} %get-tuple-element.9.coef), custom_call_target="tpu_custom_call" | custom-call | tf_op jit(solution)/shard_map/finish/pallas_call | solution.py:322
Async XLA Ops:
  2.7 19.7 %collective-permute-start.1 = (f32[40,128]{1,0:T(8,128)}, f32[40,128]{1,0:T(8,128)S(1)}, u32[]{:S(2)}, u32[]{:S(2)}) collective-permute-start(f32[40,128]{1,0:T(8,128)} %get-tuple-element.10), channel_id=1, source_target_pairs={{1,0},{2,1},{3,2},{4,3},{5,4},{6,5},{7,6},{8,7},{9,8},{10,9},{11,1... | collective-permute-start | bytes 61448 | tf_op jit(solution)/shard_map/ppermute | solution.py:308
  11.2 11.3 %collective-permute-start = (f32[40,128]{1,0:T(8,128)}, f32[40,128]{1,0:T(8,128)S(1)}, u32[]{:S(2)}, u32[]{:S(2)}) collective-permute-start(f32[40,128]{1,0:T(8,128)} %get-tuple-element.10), channel_id=1, source_target_pairs={{0,1},{1,2},{2,3},{3,4},{4,5},{5,6},{6,7},{7,8},{8,9},{9,10},{10,1... | collective-permute-start | bytes 61448 | tf_op jit(solution)/shard_map/ppermute | solution.py:307
  22.4 0.6 %copy-start = (f32[40,128]{1,0:T(8,128)}, f32[40,128]{1,0:T(8,128)S(1)}, u32[]{:S(2)}) copy-start(f32[40,128]{1,0:T(8,128)S(1)} %collective-permute-done.1.from_right) | copy-start | bytes 61444
  23.0 0.6 %copy-start.1 = (f32[40,128]{1,0:T(8,128)}, f32[40,128]{1,0:T(8,128)S(1)}, u32[]{:S(2)}) copy-start(f32[40,128]{1,0:T(8,128)S(1)} %collective-permute-done.from_left) | copy-start | bytes 61444
where the time goes:
time: 27.9 us; the launch traced here: 27.7 us
  Pallas kernels  18 us (65%)
  starting transfers between devices  8.48 us (30%)
  local copies, waits for them, and re-layouts  1.19 us (4%)
    pallas_call x1, Pallas kernels, body(): pl.pallas_call(main_kernel, out_shape=jax.ShapeDtypeStruct((BLK * TYPES,...  11.2 us
    ppermute x1, starting transfers between devices, body(): from_right = lax.ppermute(edge, 'gy', down)  8.48 us
    pallas_call x1, Pallas kernels, body(): pl.pallas_call(finish_kernel, out_shape=jax.ShapeDtypeStruct((ROWS, COLS)...  4.12 us
    pallas_call x1, Pallas kernels, body(): pl.pallas_call(edge_kernel, out_shape=(jax.ShapeDtypeStruct((40, COLS), F...  2.68 us
    unnamed x4, local copies, waits for them, and re-layouts  1.19 us
  transfers between devices with their start and end apart: 2, of which 0 were waited for; matrix products, arithmetic and copies ran while one was open for 0% of the time, Pallas kernels for 41%

commit v1 on v0

v1 whole, which is shorter than its diff:
```python
import jax
import jax.numpy as jnp
from jax import lax
from jax.experimental import pallas as pl
from jax.experimental.pallas import tpu as pltpu
from jax.sharding import PartitionSpec as P


TYPES = 4
BINS = 33
LEV = 4
BLK = 2
SUB = 2
COLS = 128
ROWS = BLK * TYPES * BINS * LEV
PAIRS = BINS * (BINS + 1) // 2
HALF = 512
TAIL = 64
KDIM = HALF + 2 * TAIL
MROWS = 80
F32 = jnp.float32
BF16 = jnp.bfloat16


def iota(shape, axis):
    return lax.broadcasted_iota(jnp.int32, shape, axis)


def split(x):
    high = x.astype(BF16)
    low = (x - high.astype(F32)).astype(BF16)
    return high, low


def block_row(t, b):
    return (b * TYPES + t) * BINS * LEV


def pair_of_column(col):
    tail = jnp.where(col >= HALF + TAIL, col - TAIL, col)
    first = jnp.where(col < HALF, col & 31, jnp.where(tail < 528, tail - HALF, tail - 528))
    second = jnp.where(
        col < HALF, (first + (col >> 5)) & 31, jnp.where(tail < 528, first + 16, BINS - 1)
    )
    low = jnp.minimum(first, second)
    high = jnp.maximum(first, second)
    pair = low * BINS - ((low * (low - 1)) >> 1) + (high - low)
    return jnp.where(tail > 560, -1, pair)


def edge_kernel(spec, sat, wind, cloudy, edge):
    lane = iota((1, COLS), 1)
    owner = ((lane + 2) & 127) >> 2
    row8 = iota((8, COLS), 0)
    main = [jnp.zeros((8, COLS), F32) for _ in range(4)]
    last = jnp.zeros((8, COLS), F32)
    for b in range(BLK):
        cloud_row = cloudy[b : b + 1, :].astype(F32)
        for l in range(LEV):
            extra = jnp.where(
                row8 == 1,
                sat[b * LEV + l : b * LEV + l + 1, :],
                jnp.where(row8 == 2, wind[b * LEV + l : b * LEV + l + 1, :], cloud_row),
            )
            for t in range(TYPES):
                spot = (t * BLK + b) * LEV + l
                mine = owner == spot
                start = block_row(t, b) + l
                for q in range(4):
                    piece = spec[pl.ds(start + 32 * q, 8, stride=LEV), :]
                    main[q] = jnp.where(mine, pltpu.roll(piece, 4 * spot, 1), main[q])
                piece = jnp.where(row8 == 0, spec[start + 128 : start + 129, :], extra)
                last = jnp.where(mine, pltpu.roll(piece, 4 * spot, 1), last)
    for q in range(4):
        edge[8 * q : 8 * q + 8, :] = main[q]
    edge[32:40, :] = last


def prepare(coll, growth, fall, lhs, coef, raw, parts):
    stacked = jnp.concatenate(
        [
            jnp.concatenate([growth[...], fall[...]], axis=0),
            jnp.zeros((COLS - 2 * TYPES, BINS), F32),
        ],
        axis=0,
    )
    stacked = jnp.concatenate([stacked, jnp.zeros((COLS, COLS - BINS), F32)], axis=1)
    turned = jnp.transpose(stacked)[0:40, :]
    for n in range(2 * TYPES):
        coef[n] = jnp.broadcast_to(turned[:, n : n + 1], (40, COLS))
    raw[...] = jnp.zeros(raw.shape, F32)
    for n in range(KDIM // COLS):
        width = min(COLS, PAIRS - COLS * n)
        for k in range(BINS):
            raw[n, TYPES * k : TYPES * k + TYPES, 0:width] = coll[k, :, COLS * n : COLS * n + width]
    for t in range(TYPES):
        for n in range(KDIM // COLS):
            rows = raw[n, pl.ds(t, 40, stride=TYPES), :]
            both = jnp.concatenate(split(rows), axis=0)
            parts[MROWS * t : MROWS * t + MROWS, COLS * n : COLS * n + COLS] = both
    wanted = pair_of_column(iota((1, KDIM), 1))
    chosen = jnp.where(iota((KDIM, KDIM), 0) == wanted, 1.0, 0.0).astype(BF16)
    lhs[...] = jnp.dot(parts[...], chosen, preferred_element_type=F32).astype(BF16)


def condense(main, top, sat, rate_main, rate_top):
    rising = jnp.maximum(sat, 0.0)
    falling = jnp.maximum(-sat, 0.0)
    transfer = rate_main * main
    up = rising * transfer
    down = falling * transfer
    down_top = falling * (rate_top * top)
    arrive_up = jnp.concatenate([jnp.zeros_like(top), up[:-1]], axis=0)
    arrive_down = jnp.concatenate([down[1:], down_top], axis=0)
    new_main = main - up - down + arrive_up + arrive_down
    new_top = top - down_top + up[-1:]
    return new_main, new_top


def pair_parts(groups, turns):
    for (main, top), turn in zip(groups, turns):
        turn[0:32, :] = main
        turn[32:48, :] = main[0:16]

    def gather(pieces):
        return jnp.concatenate(pieces, axis=1) if len(pieces) > 1 else pieces[0]

    for first in range(0, 16, 4):
        tiles = []
        for (main, _), turn in zip(groups, turns):
            parts = [
                split(main * (main if d == 0 else turn[d : d + 32, :]))
                for d in range(first, first + 4)
            ]
            tiles.append(jnp.concatenate([p[0] for p in parts] + [p[1] for p in parts], axis=0))
        columns = slice(32 * first, 32 * first + 128)
        yield (columns, columns), gather(tiles)
    tails = []
    for main, top in groups:
        square = jnp.where(iota((16, COLS), 0) == 0, top * top, 0.0)
        rest = jnp.concatenate([main[0:16] * main[16:32], main * top, square], axis=0)
        tails.append(jnp.concatenate(split(rest), axis=0))
    yield (slice(HALF, KDIM),), gather(tails)


def collect(lhs, groups, turns):
    total = None
    for columns, part in pair_parts(groups, turns):
        gain = jnp.dot(
            jnp.concatenate([lhs[:, c] for c in columns], axis=1), part, preferred_element_type=F32
        )
        total = gain if total is None else total + gain
    return total


def shares():
    x, y = lax.axis_index("gx"), lax.axis_index("gy")
    size = lax.axis_size("gy")
    odd = (y & 1) == 1
    origin = (x == 0) & (y == 0)
    total = BLK * TYPES
    first = jnp.where(odd & (y < size - 1), jnp.where(y < size // 2, 3, 1), 0)
    first = jnp.where((y == 0) & jnp.logical_not(origin), total, first)
    second = jnp.where(origin | (y == size - 1), first, total)
    return (0, first), (first, second), (second, total)


def main_kernel(which, spec, sat, cloudy, coll, growth, fall, edge, *rest):
    settled, lhs, coef = rest[-7:-4] if which < 2 else rest[-6:-3]
    turn, raw, parts = rest[-3:]
    if which < 2:
        rest[-4][...] = edge[...]
    begin, end = shares()[which]

    @pl.when((begin == 0) & (end > 0))
    def _():
        prepare(coll, growth, fall, lhs, coef, raw, parts)

    def one(n, carry):
        t = n >> 1
        b = n & 1
        start = block_row(t, b)
        left = lhs[pl.ds(pl.multiple_of(t * MROWS, 16), MROWS), :]
        rate = coef[t]
        speed = coef[TYPES + t]
        wet = cloudy[pl.ds(b, 1), :] > 0
        before = []
        state = []
        for l in range(LEV):
            main = spec[pl.ds(start + l, 32, stride=LEV), :]
            top = spec[pl.ds(start + 128 + l, 1), :]
            before.append((main, top))
            row = sat[pl.ds(b * LEV + l, 1), :]
            state.append(condense(main, top, row, rate[0:32], rate[32:33]))
        for step in range(SUB):
            for half in range(2):
                levels = range(2 * half, 2 * half + 2)
                gain = collect(
                    left,
                    [state[l] for l in levels],
                    [turn.at[LEV * step + l] for l in levels],
                )
                for k in range(2):
                    l = 2 * half + k
                    mine = gain[:, COLS * k : COLS * k + COLS]
                    main, top = state[l]
                    state[l] = (
                        main + (mine[0:32] + mine[40:72]),
                        top + (mine[32:33] + mine[72:73]),
                    )
        above = None
        for l in reversed(range(LEV)):
            main = jnp.where(wet, state[l][0], before[l][0])
            top = jnp.where(wet, state[l][1], before[l][1])
            over = (jnp.zeros_like(main), jnp.zeros_like(top)) if above is None else above
            settled[n, l, 0:32, :] = main + speed[0:32] * (over[0] - main)
            settled[n, l, 32:33, :] = top + speed[32:33] * (over[1] - top)
            above = (main, top)
        return carry

    lax.fori_loop(begin, end, one, 0)


def finish_kernel(settled, even0, odd0, even1, odd1, edge, wind, lhs, coef, out, turn, result, sems):
    lane = iota((1, COLS), 1)
    owner = ((lane + 2) & 127) >> 2
    kind = owner >> 3
    place = lane & 3
    even = even0[...] + even1[...]
    odd = odd0[...] + odd1[...]
    mine_odd = (lax.axis_index("gy") & 1) * 2
    halo = jnp.where((lane & 2) == mine_odd, even, odd)

    def by_type(pieces):
        value = pieces[0]
        for t in range(1, TYPES):
            value = jnp.where(kind == t, pieces[t], value)
        return value

    rate = by_type([coef[t] for t in range(TYPES)])
    speed = by_type([coef[TYPES + t] for t in range(TYPES)])
    main = halo[0:32]
    top = halo[32:33]
    wet = halo[35:36] > 0
    state = condense(main, top, halo[33:34], rate[0:32], rate[32:33])
    for step in range(SUB):
        gain = collect(lhs[...], [state], [turn.at[step]])
        share = by_type([gain[MROWS * t : MROWS * t + MROWS] for t in range(TYPES)])
        state = (
            state[0] + (share[0:32] + share[40:72]),
            state[1] + (share[32:33] + share[72:73]),
        )
    highest = (owner & 3) == LEV - 1

    def settle(value, speed):
        above = jnp.where(highest, 0.0, pltpu.roll(value, COLS - 4, 1))
        return value + speed * (above - value)

    ghost = jnp.concatenate(
        [
            settle(jnp.where(wet, state[0], main), speed[0:32]),
            settle(jnp.broadcast_to(jnp.where(wet, state[1], top), (8, COLS)), speed[32:40]),
        ],
        axis=0,
    )

    def weights(left, right):
        left_abs = jnp.abs(left)
        right_abs = jnp.abs(right)
        return (
            left_abs - left,
            (right - right_abs) + (7.0 * left - 3.0 * left_abs),
            1.0 - (7.0 * right - 3.0 * right_abs) + (7.0 * left + 3.0 * left_abs),
            -(7.0 * right + 3.0 * right_abs) - (left + left_abs),
            right + right_abs,
        )

    scale = 0.5 / 12.0
    far = jnp.broadcast_to(halo[34:35], (8, COLS))
    near = jnp.broadcast_to(edge[34:35], (8, COLS))
    lower = jnp.where(place == 0, pltpu.roll(far, 1, 1), pltpu.roll(near, 1, 1))
    upper = jnp.where(place == 3, pltpu.roll(far, COLS - 1, 1), pltpu.roll(near, COLS - 1, 1))
    w = weights((near + lower) * scale, (near + upper) * scale)
    weight_2 = jnp.where(place < 2, w[0], w[4])[0:1]
    weight_1 = jnp.where(place == 0, w[1], jnp.where(place == 3, w[3], 0.0))[0:1]
    by_2 = jnp.where(place < 2, pltpu.roll(ghost, 2, 1), pltpu.roll(ghost, COLS - 2, 1))
    by_1 = jnp.where(place == 0, pltpu.roll(ghost, 1, 1), pltpu.roll(ghost, COLS - 1, 1))
    extra = weight_2 * by_2 + weight_1 * by_1

    row = iota((2 * COLS, COLS), 0) & (COLS - 1)
    col = iota((2 * COLS, COLS), 1)
    shift = jnp.concatenate(
        [jnp.where(row == col + by, 1.0, 0.0).astype(BF16) for by in (-2, -1, 1, 2)], axis=1
    )
    outer = (lane < 2) | (lane >= COLS - 2)
    for b in range(BLK):
        for l in range(LEV):
            at = b * LEV + l
            own = jnp.broadcast_to(wind[at : at + 1, :], (8, COLS))
            beyond = pltpu.roll(far, (COLS - 4 * at) % COLS, 1)
            lower = pltpu.roll(jnp.where(lane == COLS - 1, beyond, own), 1, 1)
            upper = pltpu.roll(jnp.where(lane == 0, beyond, own), COLS - 1, 1)
            w = weights((own + lower) * scale, (own + upper) * scale)
            x = jnp.concatenate([settled[t * BLK + b, l] for t in range(TYPES)], axis=0)
            moved = jnp.dot(
                jnp.concatenate(split(x), axis=1), shift, preferred_element_type=F32
            )
            for t in range(TYPES):
                rows = slice(40 * t, 40 * t + 40)
                spot = (t * BLK + b) * LEV + l
                added = jnp.where(outer, pltpu.roll(extra, (COLS - 4 * spot) % COLS, 1), 0.0)
                y = w[2][0:1] * x[rows] + added
                for n, k in enumerate((0, 1, 3, 4)):
                    y = y + w[k][0:1] * moved[rows, COLS * n : COLS * n + COLS]
                start = block_row(t, b) + l
                for q in range(4):
                    result[pl.ds(start + 32 * q, 8, stride=LEV), :] = y[8 * q : 8 * q + 8]
                result[start + 128 : start + 129, :] = y[32:33]
        rows = pl.ds(b * (ROWS // BLK), ROWS // BLK)
        pltpu.make_async_copy(result.at[rows], out.at[rows], sems.at[b]).start()
    for b in range(BLK):
        rows = pl.ds(b * (ROWS // BLK), ROWS // BLK)
        pltpu.make_async_copy(result.at[rows], out.at[rows], sems.at[b]).wait()


def vmem(count):
    return [pl.BlockSpec(memory_space=pltpu.VMEM)] * count


def resident(*arrays):
    return [pltpu.with_memory_space_constraint(x, pltpu.VMEM) for x in arrays]


def swaps(pairs):
    return [(a, b) for a, b in pairs] + [(b, a) for a, b in pairs]


def body(spectra, collection, growth_rate, fall_speed, supersaturation, courant, cloudy):
    spec = spectra.reshape(ROWS, COLS)
    sat = supersaturation.reshape(BLK * LEV, COLS)
    wind = courant.reshape(BLK * LEV, COLS)
    coll = jnp.transpose(collection, (1, 0, 2))
    wide, long = lax.axis_size("gx"), lax.axis_size("gy")

    def device(x, y):
        return x * long + y % long

    early, middle, late, origin = [], [], [], []
    for x in range(wide):
        for y in range(0, long, 2):
            pair = (device(x, y), device(x, y + 1))
            (origin if x == 0 and y == 0 else early).append(pair)
            pair = (device(x, y + 1), device(x, y + 2))
            (late if y + 2 == long else middle).append(pair)

    def exchange(edge, pairs):
        return lax.ppermute(edge, ("gx", "gy"), swaps(pairs))

    edge = pl.pallas_call(
        edge_kernel,
        out_shape=pltpu.VMEM((40, COLS), F32),
        in_specs=vmem(4),
        out_specs=vmem(1)[0],
        name="edges",
    )(*resident(spec, sat, wind, cloudy))

    def blocks(which, edge, held):
        shapes = (
            pltpu.VMEM((BLK * TYPES, LEV, 40, COLS), F32),
            pltpu.VMEM((TYPES * MROWS, KDIM), BF16),
            pltpu.VMEM((2 * TYPES, 40, COLS), F32),
        )
        if which < 2:
            shapes += (pltpu.VMEM((40, COLS), F32),)
        return pl.pallas_call(
            lambda *refs: main_kernel(which, *refs),
            out_shape=shapes,
            in_specs=vmem(7 + len(held)),
            out_specs=tuple(vmem(len(shapes))),
            input_output_aliases={7 + n: n for n in range(len(held))},
            scratch_shapes=[
                pltpu.VMEM((SUB * LEV, 48, COLS), F32),
                pltpu.VMEM((KDIM // COLS, TYPES * 40, COLS), F32),
                pltpu.VMEM((TYPES * MROWS, KDIM), BF16),
            ],
        )(*resident(spec, sat, cloudy, coll, growth_rate, fall_speed, edge, *held))

    even0 = exchange(edge, early)
    *held, edge0 = blocks(0, edge, ())
    odd0 = exchange(edge0, middle)
    *held, edge1 = blocks(1, edge0, held)
    even1 = exchange(edge1, origin)
    odd1 = exchange(edge1, late)
    settled, lhs, coef = blocks(2, edge1, held)
    out = pl.pallas_call(
        finish_kernel,
        out_shape=jax.ShapeDtypeStruct((ROWS, COLS), F32),
        in_specs=vmem(9),
        out_specs=pl.BlockSpec(memory_space=pl.ANY),
        scratch_shapes=[
            pltpu.VMEM((SUB, 48, COLS), F32),
            pltpu.VMEM((ROWS, COLS), F32),
            pltpu.SemaphoreType.DMA((BLK,)),
        ],
        name="finish",
    )(*resident(settled, even0, odd0, even1, odd1, edge, wind, lhs, coef))
    return out.reshape(spectra.shape)


def solution(mesh):
    return jax.shard_map(
        body,
        mesh=mesh,
        in_specs=(
            P("gx", None, None, None, "gy"),
            P(),
            P(),
            P(),
            P("gx", None, "gy"),
            P("gx", None, "gy"),
            P("gx", "gy"),
        ),
        out_specs=P("gx", None, None, None, "gy"),
        check_vma=False,
    )
```

time: 27.9 us -> 26.3 us (0.943)
  the two profiles are of different devices: /device:TPU:62 before, /device:TPU:511 now
where the time goes in v1:
time: 26.3 us; the launch traced here: 26 us
  starting transfers between devices  12.6 us (48%)
  Pallas kernels  9.41 us (36%)
  local copies, waits for them, and re-layouts  3.81 us (14%)
    ppermute x4, starting transfers between devices, exchange(): return lax.ppermute(edge, ('gx', 'gy'), swaps(pairs))  12.6 us
    pallas_call x3, Pallas kernels, blocks(): pl.pallas_call(lambda *refs: main_kernel(which, *refs), out_shape=shapes,...  6.86 us
    unnamed x16, local copies, waits for them, and re-layouts  3.81 us
    pallas_call x1, Pallas kernels, body(): pl.pallas_call(finish_kernel, out_shape=jax.ShapeDtypeStruct((ROWS, COLS)...  2.31 us
  transfers between devices with their start and end apart: 4, of which 0 were waited for; matrix products, arithmetic and copies ran while one was open for 0% of the time, Pallas kernels for 26%

profile of v1, /device:TPU:511, one launch (start us, length us, event | category | flops | bytes accessed | tf_op | source)
XLA Modules:
  0.0 26.0 jit_solution(17691009288885697801)
XLA Ops:
  0.0 0.0 copy-start.2
  0.0 0.0 copy-start.7
  0.0 0.7 %copy-done.2 = f32[2,4,128]{2,1,0:T(4,128)S(1)} copy-done((f32[2,4,128]{2,1,0:T(4,128)S(1)}, f32[2,4,128]{2,1,0:T(4,128)}, u32[]{:S(2)}) %copy-start.2) | copy-done | bytes 4120
  0.7 0.0 copy-done.7
  0.7 0.0 copy-start
  0.7 1.0 %copy-done = f32[2,4,33,4,128]{4,3,2,1,0:T(4,128)S(1)} copy-done((f32[2,4,33,4,128]{4,3,2,1,0:T(4,128)S(1)}, f32[2,4,33,4,128]{4,3,2,1,0:T(4,128)}, u32[]{:S(2)}) %copy-start) | copy-done | bytes 540696
  1.7 0.0 copy-start.5
  1.7 0.7 %copy-done.5 = f32[2,4,128]{2,1,0:T(4,128)S(1)} copy-done((f32[2,4,128]{2,1,0:T(4,128)S(1)}, f32[2,4,128]{2,1,0:T(4,128)}, u32[]{:S(2)}) %copy-start.5) | copy-done | bytes 4120
  2.4 0.2 edges.1.refs_6_.edge
  2.7 0.7 %copy-done.1 = f32[4,33,561]{2,0,1:T(4,128)S(1)} copy-done((f32[4,33,561]{2,0,1:T(4,128)S(1)}, f32[4,33,561]{2,0,1:T(4,128)}, u32[]{:S(2)}) %copy-start.1) | copy-done | bytes 296232
  3.4 0.0 copy-done.3
  3.4 0.0 copy-done.4
  3.5 0.7 %collective-permute-start.2 = (f32[40,128]{1,0:T(8,128)S(1)}, f32[40,128]{1,0:T(8,128)S(1)}, u32[]{:S(2)}, u32[]{:S(2)}) collective-permute-start(f32[40,128]{1,0:T(8,128)S(1)} %get-tuple-element.20.refs_6_), channel_id=1, source_target_pairs={{0,1},{1,0}} | collective-permute-start | bytes 61448 | tf_op jit(solution)/shard_map/ppermute | solution.py:357
  4.1 3.2 %collective-permute-start.3 = (f32[40,128]{1,0:T(8,128)S(1)}, f32[40,128]{1,0:T(8,128)S(1)}, u32[]{:S(2)}, u32[]{:S(2)}) collective-permute-start(f32[40,128]{1,0:T(8,128)S(1)} %get-tuple-element.20.refs_6_), channel_id=1, source_target_pairs={{15,0},{31,16},{47,32},{63,48},{79,64},{95,80},{111,96},{127,112},... | collective-permute-start | bytes 61448 | tf_op jit(solution)/shard_map/ppermute | solution.py:357
  7.3 0.7 %collective-permute-start.1 = (f32[40,128]{1,0:T(8,128)S(1)}, f32[40,128]{1,0:T(8,128)S(1)}, u32[]{:S(2)}, u32[]{:S(2)}) collective-permute-start(f32[40,128]{1,0:T(8,128)S(1)} %get-tuple-element.16.refs_6_), channel_id=1, source_target_pairs={{1,2},{3,4},{5,6},{7,8},{9,10},{11,12},{13,14},{17,18},{19,20},{21... | collective-permute-start | bytes 61448 | tf_op jit(solution)/shard_map/ppermute | solution.py:357
  8.0 8.1 %collective-permute-start = (f32[40,128]{1,0:T(8,128)S(1)}, f32[40,128]{1,0:T(8,128)S(1)}, u32[]{:S(2)}, u32[]{:S(2)}) collective-permute-start(f32[40,128]{1,0:T(8,128)S(1)} %edges.1.refs_6_.edge), channel_id=1, source_target_pairs={{2,3},{4,5},{6,7},{8,9},{10,11},{12,13},{14,15},{16,17},{18,19},{2... | collective-permute-start | bytes 61448 | tf_op jit(solution)/shard_map/ppermute | solution.py:357
  16.1 6.8 %shard_map.75 = (f32[8,4,40,128]{3,2,1,0:T(8,128)S(1)}, bf16[320,640]{1,0:T(8,128)(2,1)S(1)}, f32[8,40,128]{2,1,0:T(8,128)S(1)}) custom-call(f32[1056,128]{1,0:T(8,128)S(1)} %bitcast.8, f32[8,128]{1,0:T(8,128)S(1)} %bitcast.15, s32[2,128]{1,0:T(2,128)S(1)} %copy-done.7, ...), custom_call_target="tpu_custom_call", output_to_operand_aliasing={{0}: (7, {}), {1}: (8, {}), {2}: (9, {})} | custom-call | tf_op jit(solution)/shard_map/pallas_call | solution.py:375
  23.0 0.0 copy-start.6
  23.0 0.0 collective-permute-done.2.even1
  23.0 0.0 collective-permute-done.3.odd1
  23.0 0.0 collective-permute-done.1.odd0
  23.0 0.0 collective-permute-done.even0
  23.0 0.6 %copy-done.6 = f32[2,4,128]{2,1,0:T(4,128)S(1)} copy-done((f32[2,4,128]{2,1,0:T(4,128)S(1)}, f32[2,4,128]{2,1,0:T(4,128)}, u32[]{:S(2)}) %copy-start.6) | copy-done | bytes 4120
  23.7 2.3 %finish.1 = f32[1056,128]{1,0:T(8,128)} custom-call(f32[8,4,40,128]{3,2,1,0:T(8,128)S(1)} %get-tuple-element.24.settled, f32[40,128]{1,0:T(8,128)S(1)} %collective-permute-done.even0, f32[40,128]{1,0:T(8,128)S(1)} %collective-permute-done.1.odd0, f32[40,128]{1,0:T(8,128)S(1)} %collective-permute-done.2.even1, f32[40,128]{1,0:T(8,128)S(1)} %collective-permute-done.3.odd1, ...), custom_call_target="tpu_custom_call" | custom-call | tf_op jit(solution)/shard_map/finish/pallas_call | solution.py:395
  (5 shorter events, 0.0 us)
Async XLA Ops:
  0.0 0.7 %copy-start.2 = (f32[2,4,128]{2,1,0:T(4,128)S(1)}, f32[2,4,128]{2,1,0:T(4,128)}, u32[]{:S(2)}) copy-start(f32[2,4,128]{2,1,0:T(4,128)} %param.11) | copy-start | bytes 12292
  0.0 0.7 %copy-start.7 = (s32[2,128]{1,0:T(2,128)S(1)}, s32[2,128]{1,0:T(2,128)}, u32[]{:S(2)}) copy-start(s32[2,128]{1,0:T(2,128)} %refs_2_.5) | copy-start | bytes 3076
  0.7 1.0 %copy-start = (f32[2,4,33,4,128]{4,3,2,1,0:T(4,128)S(1)}, f32[2,4,33,4,128]{4,3,2,1,0:T(4,128)}, u32[]{:S(2)}) copy-start(f32[2,4,33,4,128]{4,3,2,1,0:T(4,128)} %param.7) | copy-start | bytes 1622020
  1.7 0.7 %copy-start.5 = (f32[2,4,128]{2,1,0:T(4,128)S(1)}, f32[2,4,128]{2,1,0:T(4,128)}, u32[]{:S(2)}) copy-start(f32[2,4,128]{2,1,0:T(4,128)} %param.12) | copy-start | bytes 12292
  2.4 1.0 %copy-start.1 = (f32[4,33,561]{2,0,1:T(4,128)S(1)}, f32[4,33,561]{2,0,1:T(4,128)}, u32[]{:S(2)}) copy-start(f32[4,33,561]{2,0,1:T(4,128)} %param.8) | copy-start | bytes 888628
  2.4 1.0 %copy-start.3 = (f32[4,33]{1,0:T(4,128)S(1)}, f32[4,33]{1,0:T(4,128)}, u32[]{:S(2)}) copy-start(f32[4,33]{1,0:T(4,128)} %refs_4_.5) | copy-start | bytes 1588
  2.4 1.0 %copy-start.4 = (f32[4,33]{1,0:T(4,128)S(1)}, f32[4,33]{1,0:T(4,128)}, u32[]{:S(2)}) copy-start(f32[4,33]{1,0:T(4,128)} %refs_5_.5) | copy-start | bytes 1588
  3.5 19.5 %collective-permute-start.2 = (f32[40,128]{1,0:T(8,128)S(1)}, f32[40,128]{1,0:T(8,128)S(1)}, u32[]{:S(2)}, u32[]{:S(2)}) collective-permute-start(f32[40,128]{1,0:T(8,128)S(1)} %get-tuple-element.20.refs_6_), channel_id=1, source_target_pairs={{0,1},{1,0}} | collective-permute-start | bytes 61448 | tf_op jit(solution)/shard_map/ppermute | solution.py:357
  4.1 18.9 %collective-permute-start.3 = (f32[40,128]{1,0:T(8,128)S(1)}, f32[40,128]{1,0:T(8,128)S(1)}, u32[]{:S(2)}, u32[]{:S(2)}) collective-permute-start(f32[40,128]{1,0:T(8,128)S(1)} %get-tuple-element.20.refs_6_), channel_id=1, source_target_pairs={{15,0},{31,16},{47,32},{63,48},{79,64},{95,80},{111,96},{127,112},... | collective-permute-start | bytes 61448 | tf_op jit(solution)/shard_map/ppermute | solution.py:357
  7.3 15.7 %collective-permute-start.1 = (f32[40,128]{1,0:T(8,128)S(1)}, f32[40,128]{1,0:T(8,128)S(1)}, u32[]{:S(2)}, u32[]{:S(2)}) collective-permute-start(f32[40,128]{1,0:T(8,128)S(1)} %get-tuple-element.16.refs_6_), channel_id=1, source_target_pairs={{1,2},{3,4},{5,6},{7,8},{9,10},{11,12},{13,14},{17,18},{19,20},{21... | collective-permute-start | bytes 61448 | tf_op jit(solution)/shard_map/ppermute | solution.py:357
  8.0 15.0 %collective-permute-start = (f32[40,128]{1,0:T(8,128)S(1)}, f32[40,128]{1,0:T(8,128)S(1)}, u32[]{:S(2)}, u32[]{:S(2)}) collective-permute-start(f32[40,128]{1,0:T(8,128)S(1)} %edges.1.refs_6_.edge), channel_id=1, source_target_pairs={{2,3},{4,5},{6,7},{8,9},{10,11},{12,13},{14,15},{16,17},{18,19},{2... | collective-permute-start | bytes 61448 | tf_op jit(solution)/shard_map/ppermute | solution.py:357
  23.0 0.7 %copy-start.6 = (f32[2,4,128]{2,1,0:T(4,128)S(1)}, f32[2,4,128]{2,1,0:T(4,128)}, u32[]{:S(2)}) copy-start(f32[2,4,128]{2,1,0:T(4,128)} %param.12) | copy-start | bytes 12292

commit v2 on v1

--- a/solution.py
+++ b/solution.py
@@ -48,7 +48,17 @@
     return jnp.where(tail > 560, -1, pair)
 
 
-def edge_kernel(spec, sat, wind, cloudy, edge):
+def edge_kernel(*refs):
+    sources, edge, kept, sems = refs[:7], refs[7], refs[8:15], refs[15]
+    copies = [
+        pltpu.make_async_copy(src, dst, sems.at[n])
+        for n, (src, dst) in enumerate(zip(sources, kept))
+    ]
+    for copy in copies:
+        copy.start()
+    spec, sat, wind, cloudy = kept[:4]
+    for copy in copies[:4]:
+        copy.wait()
     lane = iota((1, COLS), 1)
     owner = ((lane + 2) & 127) >> 2
     row8 = iota((8, COLS), 0)
@@ -74,6 +84,8 @@
     for q in range(4):
         edge[8 * q : 8 * q + 8, :] = main[q]
     edge[32:40, :] = last
+    for copy in copies[4:]:
+        copy.wait()
 
 
 def prepare(coll, growth, fall, lhs, coef, raw, parts):
@@ -155,20 +167,18 @@
 
 def shares():
     x, y = lax.axis_index("gx"), lax.axis_index("gy")
-    size = lax.axis_size("gy")
-    odd = (y & 1) == 1
-    origin = (x == 0) & (y == 0)
-    total = BLK * TYPES
-    first = jnp.where(odd & (y < size - 1), jnp.where(y < size // 2, 3, 1), 0)
-    first = jnp.where((y == 0) & jnp.logical_not(origin), total, first)
-    second = jnp.where(origin | (y == size - 1), first, total)
-    return (0, first), (first, second), (second, total)
+    z = y >> 1
+    first = jnp.int32(0)
+    for n, count in enumerate((8, 7, 5, 3, 1)):
+        first = jnp.where(z == n, count, first)
+    first = jnp.where((x == 0) & (y == 0), 0, first)
+    return (0, first), (first, BLK * TYPES)
 
 
 def main_kernel(which, spec, sat, cloudy, coll, growth, fall, edge, *rest):
-    settled, lhs, coef = rest[-7:-4] if which < 2 else rest[-6:-3]
+    settled, lhs, coef = rest[-7:-4] if which == 0 else rest[-6:-3]
     turn, raw, parts = rest[-3:]
-    if which < 2:
+    if which == 0:
         rest[-4][...] = edge[...]
     begin, end = shares()[which]
 
@@ -221,15 +231,12 @@
     lax.fori_loop(begin, end, one, 0)
 
 
-def finish_kernel(settled, even0, odd0, even1, odd1, edge, wind, lhs, coef, out, turn, result, sems):
+def finish_kernel(settled, from_left, from_right, edge, wind, lhs, coef, out, turn, result, sems):
     lane = iota((1, COLS), 1)
     owner = ((lane + 2) & 127) >> 2
     kind = owner >> 3
     place = lane & 3
-    even = even0[...] + even1[...]
-    odd = odd0[...] + odd1[...]
-    mine_odd = (lax.axis_index("gy") & 1) * 2
-    halo = jnp.where((lane & 2) == mine_odd, even, odd)
+    halo = jnp.where(place < 2, from_right[...], from_left[...])
 
     def by_type(pieces):
         value = pieces[0]
@@ -331,38 +338,24 @@
     return [pltpu.with_memory_space_constraint(x, pltpu.VMEM) for x in arrays]
 
 
-def swaps(pairs):
-    return [(a, b) for a, b in pairs] + [(b, a) for a, b in pairs]
-
-
 def body(spectra, collection, growth_rate, fall_speed, supersaturation, courant, cloudy):
-    spec = spectra.reshape(ROWS, COLS)
-    sat = supersaturation.reshape(BLK * LEV, COLS)
-    wind = courant.reshape(BLK * LEV, COLS)
-    coll = jnp.transpose(collection, (1, 0, 2))
-    wide, long = lax.axis_size("gx"), lax.axis_size("gy")
-
-    def device(x, y):
-        return x * long + y % long
-
-    early, middle, late, origin = [], [], [], []
-    for x in range(wide):
-        for y in range(0, long, 2):
-            pair = (device(x, y), device(x, y + 1))
-            (origin if x == 0 and y == 0 else early).append(pair)
-            pair = (device(x, y + 1), device(x, y + 2))
-            (late if y + 2 == long else middle).append(pair)
-
-    def exchange(edge, pairs):
-        return lax.ppermute(edge, ("gx", "gy"), swaps(pairs))
-
-    edge = pl.pallas_call(
+    sources = (
+        spectra.reshape(ROWS, COLS),
+        supersaturation.reshape(BLK * LEV, COLS),
+        courant.reshape(BLK * LEV, COLS),
+        cloudy,
+        jnp.transpose(collection, (1, 0, 2)),
+        growth_rate,
+        fall_speed,
+    )
+    edge, spec, sat, wind, wet, coll, growth, fall = pl.pallas_call(
         edge_kernel,
-        out_shape=pltpu.VMEM((40, COLS), F32),
-        in_specs=vmem(4),
-        out_specs=vmem(1)[0],
+        out_shape=(pltpu.VMEM((40, COLS), F32), *(pltpu.VMEM(x.shape, x.dtype) for x in sources)),
+        in_specs=[pl.BlockSpec(memory_space=pl.ANY)] * len(sources),
+        out_specs=tuple(vmem(1 + len(sources))),
+        scratch_shapes=[pltpu.SemaphoreType.DMA((len(sources),))],
         name="edges",
-    )(*resident(spec, sat, wind, cloudy))
+    )(*sources)
 
     def blocks(which, edge, held):
         shapes = (
@@ -370,7 +363,7 @@
             pltpu.VMEM((TYPES * MROWS, KDIM), BF16),
             pltpu.VMEM((2 * TYPES, 40, COLS), F32),
         )
-        if which < 2:
+        if which == 0:
             shapes += (pltpu.VMEM((40, COLS), F32),)
         return pl.pallas_call(
             lambda *refs: main_kernel(which, *refs),
@@ -383,19 +376,19 @@
                 pltpu.VMEM((KDIM // COLS, TYPES * 40, COLS), F32),
                 pltpu.VMEM((TYPES * MROWS, KDIM), BF16),
             ],
-        )(*resident(spec, sat, cloudy, coll, growth_rate, fall_speed, edge, *held))
-
-    even0 = exchange(edge, early)
-    *held, edge0 = blocks(0, edge, ())
-    odd0 = exchange(edge0, middle)
-    *held, edge1 = blocks(1, edge0, held)
-    even1 = exchange(edge1, origin)
-    odd1 = exchange(edge1, late)
-    settled, lhs, coef = blocks(2, edge1, held)
+        )(*resident(spec, sat, wet, coll, growth, fall, edge, *held))
+
+    count = lax.axis_size("gy")
+    up = [(i, (i + 1) % count) for i in range(count)]
+    down = [(j, i) for i, j in up]
+    *held, packed = blocks(0, edge, ())
+    from_left = lax.ppermute(packed, "gy", up)
+    from_right = lax.ppermute(packed, "gy", down)
+    settled, lhs, coef = blocks(1, packed, held)
     out = pl.pallas_call(
         finish_kernel,
         out_shape=jax.ShapeDtypeStruct((ROWS, COLS), F32),
-        in_specs=vmem(9),
+        in_specs=vmem(7),
         out_specs=pl.BlockSpec(memory_space=pl.ANY),
         scratch_shapes=[
             pltpu.VMEM((SUB, 48, COLS), F32),
@@ -403,7 +396,7 @@
             pltpu.SemaphoreType.DMA((BLK,)),
         ],
         name="finish",
-    )(*resident(settled, even0, odd0, even1, odd1, edge, wind, lhs, coef))
+    )(*resident(settled, from_left, from_right, edge, wind, lhs, coef))
     return out.reshape(spectra.shape)
 
 

time: 26.3 us -> 16.7 us (0.63)
  the two profiles are of different devices: /device:TPU:511 before, /device:TPU:54 now
where the time goes in v2:
time: 16.7 us; the launch traced here: 16.6 us
  Pallas kernels  10.5 us (63%)
  waiting for transfers between devices  4.41 us (26%)
  starting transfers between devices  1.68 us (10%)
    pallas_call x2, Pallas kernels, blocks(): pl.pallas_call(lambda *refs: main_kernel(which, *refs), out_shape=shapes,...  6.84 us
    ppermute x1, waiting for transfers between devices, body(): from_left = lax.ppermute(packed, 'gy', up)  2.94 us
    pallas_call x1, Pallas kernels, body(): pl.pallas_call(finish_kernel, out_shape=jax.ShapeDtypeStruct((ROWS, COLS)...  2.31 us
    ppermute x1, starting transfers between devices, body(): from_right = lax.ppermute(packed, 'gy', down)  1.68 us
    ppermute x1, waiting for transfers between devices, body(): from_right = lax.ppermute(packed, 'gy', down)  1.48 us
    pallas_call x1, Pallas kernels, body(): pl.pallas_call(edge_kernel, out_shape=(pltpu.VMEM((40, COLS), F32), *(plt...  1.35 us
  transfers between devices with their start and end apart: 2, of which 2 were waited for; matrix products, arithmetic and copies ran while one was open for 0% of the time, Pallas kernels for 0%

profile of v2, /device:TPU:54, one launch (start us, length us, event | category | flops | bytes accessed | tf_op | source)
XLA Modules:
  0.0 16.6 jit_solution(18403686630909040958)
XLA Ops:
  0.0 1.3 %edges.1 = (f32[40,128]{1,0:T(8,128)S(1)}, f32[1056,128]{1,0:T(8,128)S(1)}, f32[8,128]{1,0:T(8,128)S(1)}, f32[8,128]{1,0:T(8,128)S(1)}, s32[2,128]{1,0:T(2,128)S...) custom-call(f32[1056,128]{1,0:T(8,128)} %bitcast.5, f32[8,128]{1,0:T(8,128)} %bitcast.7, ...), custom_call_target="tpu_custom_call" | custom-call | tf_op jit(solution)/shard_map/edges/pallas_call | solution.py:351
  1.4 6.8 %shard_map.73 = (f32[8,4,40,128]{3,2,1,0:T(8,128)S(1)}, bf16[320,640]{1,0:T(8,128)(2,1)S(1)}, f32[8,40,128]{2,1,0:T(8,128)S(1)}, f32[40,128]{1,0:T(8,128)S(1)}) custom-call(f32[1056,128]{1,0:T(8,128)S(1)} %get-tuple-element.20.refs_0_, f32[8,128]{1,0:T(8,128)S(1)} %get-tuple-element.21.refs_1_, s32[2,128]{1,0:T(2,128)S(1)} %get-tuple-element.22.refs_2_, ...), custom_call_target="tpu_custom_call" | custom-call | tf_op jit(solution)/shard_map/pallas_call | solution.py:368
  8.2 1.7 %collective-permute-start.1 = (f32[40,128]{1,0:T(8,128)S(1)}, f32[40,128]{1,0:T(8,128)S(1)}, u32[]{:S(2)}, u32[]{:S(2)}) collective-permute-start(f32[40,128]{1,0:T(8,128)S(1)} %get-tuple-element.27.refs_6_), channel_id=1, source_target_pairs={{1,0},{2,1},{3,2},{4,3},{5,4},{6,5},{7,6},{8,7},{9,8},{10,9},{11,1... | collective-permute-start | bytes 61448 | tf_op jit(solution)/shard_map/ppermute | solution.py:386
  9.9 0.0 collective-permute-start
  9.9 1.5 %collective-permute-done.1.from_right = f32[40,128]{1,0:T(8,128)S(1)} collective-permute-done((f32[40,128]{1,0:T(8,128)S(1)}, f32[40,128]{1,0:T(8,128)S(1)}, u32[]{:S(2)}, u32[]{:S(2)}) %collective-permute-start.1) | collective-permute-done | bytes 20512 | tf_op jit(solution)/shard_map/ppermute | solution.py:386
  11.4 2.9 %collective-permute-done.from_left = f32[40,128]{1,0:T(8,128)S(1)} collective-permute-done((f32[40,128]{1,0:T(8,128)S(1)}, f32[40,128]{1,0:T(8,128)S(1)}, u32[]{:S(2)}, u32[]{:S(2)}) %collective-permute-start) | collective-permute-done | bytes 20512 | tf_op jit(solution)/shard_map/ppermute | solution.py:385
  14.3 2.3 %finish.1 = f32[1056,128]{1,0:T(8,128)} custom-call(f32[8,4,40,128]{3,2,1,0:T(8,128)S(1)} %get-tuple-element.31.settled, f32[40,128]{1,0:T(8,128)S(1)} %collective-permute-done.from_left, f32[40,128]{1,0:T(8,128)S(1)} %collective-permute-done.1.from_right, f32[40,128]{1,0:T(8,128)S(1)} %get-tuple-element.26.refs_6_.edge, ...), custom_call_target="tpu_custom_call" | custom-call | tf_op jit(solution)/shard_map/finish/pallas_call | solution.py:388
  (1 shorter events, 0.0 us)
Async XLA Ops:
  8.2 3.2 %collective-permute-start.1 = (f32[40,128]{1,0:T(8,128)S(1)}, f32[40,128]{1,0:T(8,128)S(1)}, u32[]{:S(2)}, u32[]{:S(2)}) collective-permute-start(f32[40,128]{1,0:T(8,128)S(1)} %get-tuple-element.27.refs_6_), channel_id=1, source_target_pairs={{1,0},{2,1},{3,2},{4,3},{5,4},{6,5},{7,6},{8,7},{9,8},{10,9},{11,1... | collective-permute-start | bytes 61448 | tf_op jit(solution)/shard_map/ppermute | solution.py:386
  9.9 4.4 %collective-permute-start = (f32[40,128]{1,0:T(8,128)S(1)}, f32[40,128]{1,0:T(8,128)S(1)}, u32[]{:S(2)}, u32[]{:S(2)}) collective-permute-start(f32[40,128]{1,0:T(8,128)S(1)} %get-tuple-element.27.refs_6_), channel_id=1, source_target_pairs={{0,1},{1,2},{2,3},{3,4},{4,5},{5,6},{6,7},{7,8},{8,9},{9,10},{10,1... | collective-permute-start | bytes 61448 | tf_op jit(solution)/shard_map/ppermute | solution.py:385

commit v3 on v2

--- a/solution.py
+++ b/solution.py
@@ -18,6 +18,7 @@
 TAIL = 64
 KDIM = HALF + 2 * TAIL
 MROWS = 80
+SCALE = 0.5 / 12.0
 F32 = jnp.float32
 BF16 = jnp.bfloat16
 
@@ -49,15 +50,19 @@
 
 
 def edge_kernel(*refs):
-    sources, edge, kept, sems = refs[:7], refs[7], refs[8:15], refs[15]
-    copies = [
-        pltpu.make_async_copy(src, dst, sems.at[n])
-        for n, (src, dst) in enumerate(zip(sources, kept))
-    ]
-    for copy in copies:
-        copy.start()
+    sources, edge, chosen, kept, sems = refs[:7], refs[7], refs[8], refs[9:16], refs[16]
+    halves = [pl.ds(b * (ROWS // BLK), ROWS // BLK) for b in range(BLK)]
+    pairs = [(sources[0].at[rows], kept[0].at[rows]) for rows in halves]
+    pairs += list(zip(sources[1:], kept[1:]))
+    copies = [pltpu.make_async_copy(*pair, sems.at[n]) for n, pair in enumerate(pairs)]
+    for n in (2, 3, 4, 0, 1, 5, 6, 7):
+        copies[n].start()
+    wanted = pair_of_column(iota((1, KDIM), 1))
+    for first in range(0, KDIM, COLS):
+        rows = iota((COLS, KDIM), 0) + first
+        chosen[first : first + COLS, :] = jnp.where(rows == wanted, 1.0, 0.0).astype(BF16)
     spec, sat, wind, cloudy = kept[:4]
-    for copy in copies[:4]:
+    for copy in copies[2:5]:
         copy.wait()
     lane = iota((1, COLS), 1)
     owner = ((lane + 2) & 127) >> 2
@@ -65,6 +70,7 @@
     main = [jnp.zeros((8, COLS), F32) for _ in range(4)]
     last = jnp.zeros((8, COLS), F32)
     for b in range(BLK):
+        copies[b].wait()
         cloud_row = cloudy[b : b + 1, :].astype(F32)
         for l in range(LEV):
             extra = jnp.where(
@@ -84,11 +90,23 @@
     for q in range(4):
         edge[8 * q : 8 * q + 8, :] = main[q]
     edge[32:40, :] = last
-    for copy in copies[4:]:
+    for copy in copies[5:]:
         copy.wait()
 
 
-def prepare(coll, growth, fall, lhs, coef, raw, parts):
+def weights(left, right):
+    left_abs = jnp.abs(left)
+    right_abs = jnp.abs(right)
+    return (
+        left_abs - left,
+        (right - right_abs) + (7.0 * left - 3.0 * left_abs),
+        1.0 - (7.0 * right - 3.0 * right_abs) + (7.0 * left + 3.0 * left_abs),
+        -(7.0 * right + 3.0 * right_abs) - (left + left_abs),
+        right + right_abs,
+    )
+
+
+def prepare(coll, growth, fall, wind, chosen, lhs, coef, stencil, raw, parts):
     stacked = jnp.concatenate(
         [
             jnp.concatenate([growth[...], fall[...]], axis=0),
@@ -100,6 +118,13 @@
     turned = jnp.transpose(stacked)[0:40, :]
     for n in range(2 * TYPES):
         coef[n] = jnp.broadcast_to(turned[:, n : n + 1], (40, COLS))
+    lane = iota((1, COLS), 1)
+    own = wind[...]
+    left = jnp.where(lane == 0, 0.0, (own + pltpu.roll(own, 1, 1)) * SCALE)
+    right = jnp.where(lane == COLS - 1, 0.0, (own + pltpu.roll(own, COLS - 1, 1)) * SCALE)
+    for by, value in zip(range(-2, 3), weights(left, right)):
+        inside = (lane + by >= 0) & (lane + by < COLS)
+        stencil[by + 2] = jnp.where(inside, value, 0.0)
     raw[...] = jnp.zeros(raw.shape, F32)
     for n in range(KDIM // COLS):
         width = min(COLS, PAIRS - COLS * n)
@@ -110,9 +135,7 @@
             rows = raw[n, pl.ds(t, 40, stride=TYPES), :]
             both = jnp.concatenate(split(rows), axis=0)
             parts[MROWS * t : MROWS * t + MROWS, COLS * n : COLS * n + COLS] = both
-    wanted = pair_of_column(iota((1, KDIM), 1))
-    chosen = jnp.where(iota((KDIM, KDIM), 0) == wanted, 1.0, 0.0).astype(BF16)
-    lhs[...] = jnp.dot(parts[...], chosen, preferred_element_type=F32).astype(BF16)
+    lhs[...] = jnp.dot(parts[...], chosen[...], preferred_element_type=F32).astype(BF16)
 
 
 def condense(main, top, sat, rate_main, rate_top):
@@ -165,6 +188,25 @@
     return total
 
 
+def collect_apart(lhs, main, top, turn):
+    turn[0:32, :] = main
+    turn[32:48, :] = main[0:16]
+    total = None
+    for first in range(0, 16, 8):
+        value = jnp.concatenate(
+            [main * (main if d == 0 else turn[d : d + 32, :]) for d in range(first, first + 8)],
+            axis=0,
+        )
+        part = jnp.concatenate(split(value), axis=1)
+        gain = jnp.dot(lhs[:, 32 * first : 32 * first + 256], part, preferred_element_type=F32)
+        total = gain if total is None else total + gain
+    square = jnp.where(iota((16, COLS), 0) == 0, top * top, 0.0)
+    rest = jnp.concatenate([main[0:16] * main[16:32], main * top, square], axis=0)
+    part = jnp.concatenate(split(rest), axis=1)
+    total = total + jnp.dot(lhs[:, HALF : HALF + TAIL], part, preferred_element_type=F32)
+    return total[:, 0:COLS] + total[:, COLS : 2 * COLS]
+
+
 def shares():
     x, y = lax.axis_index("gx"), lax.axis_index("gy")
     z = y >> 1
@@ -175,18 +217,36 @@
     return (0, first), (first, BLK * TYPES)
 
 
-def main_kernel(which, spec, sat, cloudy, coll, growth, fall, edge, *rest):
-    settled, lhs, coef = rest[-7:-4] if which == 0 else rest[-6:-3]
-    turn, raw, parts = rest[-3:]
+def main_kernel(which, spec, sat, wind, cloudy, coll, growth, fall, chosen, edge, *rest):
+    result, rim, lhs, coef, stencil = rest[-10:-5] if which == 0 else rest[-9:-4]
+    turn, raw, parts, held = rest[-4:]
     if which == 0:
-        rest[-4][...] = edge[...]
+        rest[-5][...] = edge[...]
     begin, end = shares()[which]
+    owner = ((iota((1, COLS), 1) + 2) & (COLS - 1)) >> 2
 
     @pl.when((begin == 0) & (end > 0))
     def _():
-        prepare(coll, growth, fall, lhs, coef, raw, parts)
+        prepare(coll, growth, fall, wind, chosen, lhs, coef, stencil, raw, parts)
+
+    def advect(n):
+        t = n >> 1
+        b = n & 1
+        start = block_row(t, b)
+        for l in range(LEV):
+            settled = held[l]
+            spot = n * LEV + l
+            rim[...] = jnp.where(owner == spot, pltpu.roll(settled, 4 * spot, 1), rim[...])
+            w = [stencil[k, pl.ds(b * LEV + l, 1), :] for k in range(5)]
+            y = w[2] * settled
+            for by in (-2, -1, 1, 2):
+                y = y + w[by + 2] * pltpu.roll(settled, (COLS - by) % COLS, 1)
+            for q in range(4):
+                result[pl.ds(start + l + 32 * q, 8, stride=LEV), :] = y[8 * q : 8 * q + 8]
+            result[pl.ds(start + l + 128, 1), :] = y[32:33]
 
     def one(n, carry):
+        advect(jnp.maximum(n - 1, begin))
         t = n >> 1
         b = n & 1
         start = block_row(t, b)
@@ -223,15 +283,19 @@
             main = jnp.where(wet, state[l][0], before[l][0])
             top = jnp.where(wet, state[l][1], before[l][1])
             over = (jnp.zeros_like(main), jnp.zeros_like(top)) if above is None else above
-            settled[n, l, 0:32, :] = main + speed[0:32] * (over[0] - main)
-            settled[n, l, 32:33, :] = top + speed[32:33] * (over[1] - top)
+            held[l, 0:32, :] = main + speed[0:32] * (over[0] - main)
+            held[l, 32:40, :] = jnp.broadcast_to(top + speed[32:33] * (over[1] - top), (8, COLS))
             above = (main, top)
         return carry
 
     lax.fori_loop(begin, end, one, 0)
 
-
-def finish_kernel(settled, from_left, from_right, edge, wind, lhs, coef, out, turn, result, sems):
+    @pl.when(end > begin)
+    def _():
+        advect(end - 1)
+
+
+def finish_kernel(result, rim, from_left, from_right, edge, lhs, coef, out, turn, final, sems):
     lane = iota((1, COLS), 1)
     owner = ((lane + 2) & 127) >> 2
     kind = owner >> 3
@@ -251,7 +315,7 @@
     wet = halo[35:36] > 0
     state = condense(main, top, halo[33:34], rate[0:32], rate[32:33])
     for step in range(SUB):
-        gain = collect(lhs[...], [state], [turn.at[step]])
+        gain = collect_apart(lhs, *state, turn.at[step])
         share = by_type([gain[MROWS * t : MROWS * t + MROWS] for t in range(TYPES)])
         state = (
             state[0] + (share[0:32] + share[40:72]),
@@ -271,63 +335,53 @@
         axis=0,
     )
 
-    def weights(left, right):
-        left_abs = jnp.abs(left)
-        right_abs = jnp.abs(right)
-        return (
-            left_abs - left,
-            (right - right_abs) + (7.0 * left - 3.0 * left_abs),
-            1.0 - (7.0 * right - 3.0 * right_abs) + (7.0 * left + 3.0 * left_abs),
-            -(7.0 * right + 3.0 * right_abs) - (left + left_abs),
-            right + right_abs,
-        )
-
-    scale = 0.5 / 12.0
     far = jnp.broadcast_to(halo[34:35], (8, COLS))
     near = jnp.broadcast_to(edge[34:35], (8, COLS))
     lower = jnp.where(place == 0, pltpu.roll(far, 1, 1), pltpu.roll(near, 1, 1))
     upper = jnp.where(place == 3, pltpu.roll(far, COLS - 1, 1), pltpu.roll(near, COLS - 1, 1))
-    w = weights((near + lower) * scale, (near + upper) * scale)
-    weight_2 = jnp.where(place < 2, w[0], w[4])[0:1]
-    weight_1 = jnp.where(place == 0, w[1], jnp.where(place == 3, w[3], 0.0))[0:1]
-    by_2 = jnp.where(place < 2, pltpu.roll(ghost, 2, 1), pltpu.roll(ghost, COLS - 2, 1))
-    by_1 = jnp.where(place == 0, pltpu.roll(ghost, 1, 1), pltpu.roll(ghost, COLS - 1, 1))
-    extra = weight_2 * by_2 + weight_1 * by_1
-
-    row = iota((2 * COLS, COLS), 0) & (COLS - 1)
-    col = iota((2 * COLS, COLS), 1)
-    shift = jnp.concatenate(
-        [jnp.where(row == col + by, 1.0, 0.0).astype(BF16) for by in (-2, -1, 1, 2)], axis=1
-    )
+    left = (near + lower) * SCALE
+    right = (near + upper) * SCALE
+    left_abs = jnp.abs(left)
+    right_abs = jnp.abs(right)
+
+    def by_place(first, second, third, fourth):
+        value = jnp.where(place == 0, first, jnp.where(place == 3, fourth, 0.0))
+        return jnp.where(place == 1, second, jnp.where(place == 2, third, value))[0:1]
+
+    own_0 = by_place(7.0 * left + 3.0 * left_abs, 0.0, 0.0, -(7.0 * right - 3.0 * right_abs))
+    own_1 = by_place(-(left + left_abs), 0.0, 0.0, right - right_abs)
+    halo_1 = by_place(
+        (7.0 * left - 3.0 * left_abs) + (right - right_abs),
+        0.0,
+        0.0,
+        -(7.0 * right + 3.0 * right_abs) - (left + left_abs),
+    )
+    halo_2 = by_place(
+        left_abs - left, left_abs - left, right + right_abs, right + right_abs
+    )
+    inner = rim[...]
+    inner_1 = jnp.where(place == 0, pltpu.roll(inner, COLS - 1, 1), pltpu.roll(inner, 1, 1))
+    ghost_1 = jnp.where(place == 0, pltpu.roll(ghost, 1, 1), pltpu.roll(ghost, COLS - 1, 1))
+    ghost_2 = jnp.where(place < 2, pltpu.roll(ghost, 2, 1), pltpu.roll(ghost, COLS - 2, 1))
+    extra = own_0 * inner + own_1 * inner_1 + halo_1 * ghost_1 + halo_2 * ghost_2
+
     outer = (lane < 2) | (lane >= COLS - 2)
     for b in range(BLK):
-        for l in range(LEV):
-            at = b * LEV + l
-            own = jnp.broadcast_to(wind[at : at + 1, :], (8, COLS))
-            beyond = pltpu.roll(far, (COLS - 4 * at) % COLS, 1)
-            lower = pltpu.roll(jnp.where(lane == COLS - 1, beyond, own), 1, 1)
-            upper = pltpu.roll(jnp.where(lane == 0, beyond, own), COLS - 1, 1)
-            w = weights((own + lower) * scale, (own + upper) * scale)
-            x = jnp.concatenate([settled[t * BLK + b, l] for t in range(TYPES)], axis=0)
-            moved = jnp.dot(
-                jnp.concatenate(split(x), axis=1), shift, preferred_element_type=F32
-            )
-            for t in range(TYPES):
-                rows = slice(40 * t, 40 * t + 40)
+        for t in range(TYPES):
+            for l in range(LEV):
                 spot = (t * BLK + b) * LEV + l
                 added = jnp.where(outer, pltpu.roll(extra, (COLS - 4 * spot) % COLS, 1), 0.0)
-                y = w[2][0:1] * x[rows] + added
-                for n, k in enumerate((0, 1, 3, 4)):
-                    y = y + w[k][0:1] * moved[rows, COLS * n : COLS * n + COLS]
                 start = block_row(t, b) + l
                 for q in range(4):
-                    result[pl.ds(start + 32 * q, 8, stride=LEV), :] = y[8 * q : 8 * q + 8]
-                result[start + 128 : start + 129, :] = y[32:33]
+                    rows = pl.ds(start + 32 * q, 8, stride=LEV)
+                    final[rows, :] = result[rows, :] + added[8 * q : 8 * q + 8]
+                rows = slice(start + 128, start + 129)
+                final[rows, :] = result[rows, :] + added[32:33]
         rows = pl.ds(b * (ROWS // BLK), ROWS // BLK)
-        pltpu.make_async_copy(result.at[rows], out.at[rows], sems.at[b]).start()
+        pltpu.make_async_copy(final.at[rows], out.at[rows], sems.at[b]).start()
     for b in range(BLK):
         rows = pl.ds(b * (ROWS // BLK), ROWS // BLK)
-        pltpu.make_async_copy(result.at[rows], out.at[rows], sems.at[b]).wait()
+        pltpu.make_async_copy(final.at[rows], out.at[rows], sems.at[b]).wait()
 
 
 def vmem(count):
@@ -348,35 +402,42 @@
         growth_rate,
         fall_speed,
     )
-    edge, spec, sat, wind, wet, coll, growth, fall = pl.pallas_call(
+    edge, chosen, spec, sat, wind, wet, coll, growth, fall = pl.pallas_call(
         edge_kernel,
-        out_shape=(pltpu.VMEM((40, COLS), F32), *(pltpu.VMEM(x.shape, x.dtype) for x in sources)),
+        out_shape=(
+            pltpu.VMEM((40, COLS), F32),
+            pltpu.VMEM((KDIM, KDIM), BF16),
+            *(pltpu.VMEM(x.shape, x.dtype) for x in sources),
+        ),
         in_specs=[pl.BlockSpec(memory_space=pl.ANY)] * len(sources),
-        out_specs=tuple(vmem(1 + len(sources))),
-        scratch_shapes=[pltpu.SemaphoreType.DMA((len(sources),))],
+        out_specs=tuple(vmem(2 + len(sources))),
+        scratch_shapes=[pltpu.SemaphoreType.DMA((1 + len(sources),))],
         name="edges",
     )(*sources)
 
     def blocks(which, edge, held):
         shapes = (
-            pltpu.VMEM((BLK * TYPES, LEV, 40, COLS), F32),
+            pltpu.VMEM((ROWS, COLS), F32),
+            pltpu.VMEM((40, COLS), F32),
             pltpu.VMEM((TYPES * MROWS, KDIM), BF16),
             pltpu.VMEM((2 * TYPES, 40, COLS), F32),
+            pltpu.VMEM((5, BLK * LEV, COLS), F32),
         )
         if which == 0:
             shapes += (pltpu.VMEM((40, COLS), F32),)
         return pl.pallas_call(
             lambda *refs: main_kernel(which, *refs),
             out_shape=shapes,
-            in_specs=vmem(7 + len(held)),
+            in_specs=vmem(9 + len(held)),
             out_specs=tuple(vmem(len(shapes))),
-            input_output_aliases={7 + n: n for n in range(len(held))},
+            input_output_aliases={9 + n: n for n in range(len(held))},
             scratch_shapes=[
                 pltpu.VMEM((SUB * LEV, 48, COLS), F32),
                 pltpu.VMEM((KDIM // COLS, TYPES * 40, COLS), F32),
                 pltpu.VMEM((TYPES * MROWS, KDIM), BF16),
+                pltpu.VMEM((LEV, 40, COLS), F32),
             ],
-        )(*resident(spec, sat, wet, coll, growth, fall, edge, *held))
+        )(*resident(spec, sat, wind, wet, coll, growth, fall, chosen, edge, *held))
 
     count = lax.axis_size("gy")
     up = [(i, (i + 1) % count) for i in range(count)]
@@ -384,7 +445,7 @@
     *held, packed = blocks(0, edge, ())
     from_left = lax.ppermute(packed, "gy", up)
     from_right = lax.ppermute(packed, "gy", down)
-    settled, lhs, coef = blocks(1, packed, held)
+    result, rim, lhs, coef, _ = blocks(1, packed, held)
     out = pl.pallas_call(
         finish_kernel,
         out_shape=jax.ShapeDtypeStruct((ROWS, COLS), F32),
@@ -396,7 +457,7 @@
             pltpu.SemaphoreType.DMA((BLK,)),
         ],
         name="finish",
-    )(*resident(settled, from_left, from_right, edge, wind, lhs, coef))
+    )(*resident(result, rim, from_left, from_right, edge, lhs, coef))
     return out.reshape(spectra.shape)
 
 

time: 16.7 us -> 19.6 us (1.17)
  the two profiles are of different devices: /device:TPU:54 before, /device:TPU:0 now
where the time goes in v3:
time: 19.6 us; the launch traced here: 19.4 us
  Pallas kernels  10.5 us (54%)
  local copies, waits for them, and re-layouts  5.68 us (29%)
  starting transfers between devices  3.14 us (16%)
    pallas_call x2, Pallas kernels, blocks(): pl.pallas_call(lambda *refs: main_kernel(which, *refs), out_shape=shapes,...  7.13 us
    unnamed x12, local copies, waits for them, and re-layouts  5.68 us
    ppermute x1, starting transfers between devices, body(): from_right = lax.ppermute(packed, 'gy', down)  3.13 us
    pallas_call x1, Pallas kernels, body(): pl.pallas_call(finish_kernel, out_shape=jax.ShapeDtypeStruct((ROWS, COLS)...  2.01 us
    pallas_call x1, Pallas kernels, body(): pl.pallas_call(edge_kernel, out_shape=(pltpu.VMEM((40, COLS), F32), pltpu...  1.38 us
  transfers between devices with their start and end apart: 2, of which 0 were waited for; matrix products, arithmetic and copies ran while one was open for 0% of the time, Pallas kernels for 37%

profile of v3, /device:TPU:0, one launch (start us, length us, event | category | flops | bytes accessed | tf_op | source)
XLA Modules:
  0.0 19.4 jit_solution(1622473640640970550)
XLA Ops:
  0.0 1.4 %edges.1 = (f32[40,128]{1,0:T(8,128)S(1)}, bf16[640,640]{1,0:T(8,128)(2,1)S(1)}, f32[1056,128]{1,0:T(8,128)S(1)}, f32[8,128]{1,0:T(8,128)S(1)}, f32[8,128]{1,0:T...) custom-call(f32[1056,128]{1,0:T(8,128)} %bitcast.5, ...), custom_call_target="tpu_custom_call" | custom-call | tf_op jit(solution)/shard_map/edges/pallas_call | solution.py:405
  1.4 0.0 copy-start
  1.4 0.8 %copy-done = bf16[640,640]{1,0:T(8,128)(2,1)} copy-done((bf16[640,640]{1,0:T(8,128)(2,1)}, bf16[640,640]{1,0:T(8,128)(2,1)S(1)}, u32[]{:S(2)}) %copy-start) | copy-done | bytes 819224
  2.3 0.0 copy-start.2
  2.3 0.8 %copy-done.2 = f32[1056,128]{1,0:T(8,128)} copy-done((f32[1056,128]{1,0:T(8,128)}, f32[1056,128]{1,0:T(8,128)S(1)}, u32[]{:S(2)}) %copy-start.2) | copy-done | bytes 540696
  3.1 3.1 %collective-permute-start.1 = (f32[40,128]{1,0:T(8,128)S(1)}, f32[40,128]{1,0:T(8,128)S(1)}, u32[]{:S(2)}, u32[]{:S(2)}) collective-permute-start(f32[40,128]{1,0:T(8,128)S(1)} %get-tuple-element.33.refs_8_), channel_id=1, source_target_pairs={{1,0},{2,1},{3,2},{4,3},{5,4},{6,5},{7,6},{8,7},{9,8},{10,9},{11,1... | collective-permute-start | bytes 61448 | tf_op jit(solution)/shard_map/ppermute | solution.py:447
  6.2 0.0 collective-permute-start
  6.2 0.0 copy-start.1
  6.2 1.1 %copy-done.1 = bf16[640,640]{1,0:T(8,128)(2,1)S(1)} copy-done((bf16[640,640]{1,0:T(8,128)(2,1)S(1)}, bf16[640,640]{1,0:T(8,128)(2,1)}, u32[]{:S(2)}) %copy-start.1) | copy-done | bytes 819224
  7.4 0.0 copy-start.3
  7.4 1.0 %copy-done.3 = f32[1056,128]{1,0:T(8,128)S(1)} copy-done((f32[1056,128]{1,0:T(8,128)S(1)}, f32[1056,128]{1,0:T(8,128)}, u32[]{:S(2)}) %copy-start.3) | copy-done | bytes 540696
  8.4 7.1 %shard_map.74 = (f32[1056,128]{1,0:T(8,128)S(1)}, f32[40,128]{1,0:T(8,128)S(1)}, bf16[320,640]{1,0:T(8,128)(2,1)S(1)}, f32[8,40,128]{2,1,0:T(8,128)S(1)}, f32[5,8,128]{2,1,0:T(8,128)S(1)}) custom-call(f32[1056,128]{1,0:T(8,128)S(1)} %get-tuple-element.24.refs_0_, ...), custom_call_target="tpu_custom_call", output_to_operand_aliasing={{0}: (9, {}), {1}: (10, {}), {2}: (11, {}), {3}: (12, {}), ... | custom-call | tf_op jit(solution)/shard_map/pallas_call | solution.py:428
  15.5 0.0 copy-start.4
  15.5 0.8 %copy-done.4 = f32[1056,128]{1,0:T(8,128)} copy-done((f32[1056,128]{1,0:T(8,128)}, f32[1056,128]{1,0:T(8,128)S(1)}, u32[]{:S(2)}) %copy-start.4) | copy-done | bytes 540696
  16.3 0.0 collective-permute-done.1.from_right
  16.3 0.0 collective-permute-done.from_left
  16.3 0.0 copy-start.5
  16.3 1.0 %copy-done.5 = f32[1056,128]{1,0:T(8,128)S(1)} copy-done((f32[1056,128]{1,0:T(8,128)S(1)}, f32[1056,128]{1,0:T(8,128)}, u32[]{:S(2)}) %copy-start.5) | copy-done | bytes 540696
  17.4 2.0 %finish.1 = f32[1056,128]{1,0:T(8,128)} custom-call(f32[1056,128]{1,0:T(8,128)S(1)} %copy-done.5, f32[40,128]{1,0:T(8,128)S(1)} %get-tuple-element.40.rim, f32[40,128]{1,0:T(8,128)S(1)} %collective-permute-done.from_left, f32[40,128]{1,0:T(8,128)S(1)} %collective-permute-done.1.from_right, f32[40,128]{1,0:T(8,128)S(1)} %get-tuple-element.32.refs_8_.edge, ...), custom_call_target="tpu_custom_call" | custom-call | tf_op jit(solution)/shard_map/finish/pallas_call | solution.py:449
  (1 shorter events, 0.0 us)
Async XLA Ops:
  1.4 0.9 %copy-start = (bf16[640,640]{1,0:T(8,128)(2,1)}, bf16[640,640]{1,0:T(8,128)(2,1)S(1)}, u32[]{:S(2)}) copy-start(bf16[640,640]{1,0:T(8,128)(2,1)S(1)} %get-tuple-element.31.refs_7_) | copy-start | bytes 2457604
  2.3 0.8 %copy-start.2 = (f32[1056,128]{1,0:T(8,128)}, f32[1056,128]{1,0:T(8,128)S(1)}, u32[]{:S(2)}) copy-start(f32[1056,128]{1,0:T(8,128)S(1)} %get-tuple-element.34.refs_9_) | copy-start | bytes 1622020
  3.1 13.2 %collective-permute-start.1 = (f32[40,128]{1,0:T(8,128)S(1)}, f32[40,128]{1,0:T(8,128)S(1)}, u32[]{:S(2)}, u32[]{:S(2)}) collective-permute-start(f32[40,128]{1,0:T(8,128)S(1)} %get-tuple-element.33.refs_8_), channel_id=1, source_target_pairs={{1,0},{2,1},{3,2},{4,3},{5,4},{6,5},{7,6},{8,7},{9,8},{10,9},{11,1... | collective-permute-start | bytes 61448 | tf_op jit(solution)/shard_map/ppermute | solution.py:447
  6.2 10.1 %collective-permute-start = (f32[40,128]{1,0:T(8,128)S(1)}, f32[40,128]{1,0:T(8,128)S(1)}, u32[]{:S(2)}, u32[]{:S(2)}) collective-permute-start(f32[40,128]{1,0:T(8,128)S(1)} %get-tuple-element.33.refs_8_), channel_id=1, source_target_pairs={{0,1},{1,2},{2,3},{3,4},{4,5},{5,6},{6,7},{7,8},{8,9},{9,10},{10,1... | collective-permute-start | bytes 61448 | tf_op jit(solution)/shard_map/ppermute | solution.py:446
  6.2 1.1 %copy-start.1 = (bf16[640,640]{1,0:T(8,128)(2,1)S(1)}, bf16[640,640]{1,0:T(8,128)(2,1)}, u32[]{:S(2)}) copy-start(bf16[640,640]{1,0:T(8,128)(2,1)} %copy-done) | copy-start | bytes 2457604
  7.4 1.0 %copy-start.3 = (f32[1056,128]{1,0:T(8,128)S(1)}, f32[1056,128]{1,0:T(8,128)}, u32[]{:S(2)}) copy-start(f32[1056,128]{1,0:T(8,128)} %copy-done.2) | copy-start | bytes 1622020
  15.5 0.8 %copy-start.4 = (f32[1056,128]{1,0:T(8,128)}, f32[1056,128]{1,0:T(8,128)S(1)}, u32[]{:S(2)}) copy-start(f32[1056,128]{1,0:T(8,128)S(1)} %get-tuple-element.39.result) | copy-start | bytes 1622020
  16.3 1.0 %copy-start.5 = (f32[1056,128]{1,0:T(8,128)S(1)}, f32[1056,128]{1,0:T(8,128)}, u32[]{:S(2)}) copy-start(f32[1056,128]{1,0:T(8,128)} %copy-done.4) | copy-start | bytes 1622020

commit v4 on v3

--- a/solution.py
+++ b/solution.py
@@ -19,6 +19,7 @@
 KDIM = HALF + 2 * TAIL
 MROWS = 80
 SCALE = 0.5 / 12.0
+LIMIT = 16 << 20
 F32 = jnp.float32
 BF16 = jnp.bfloat16
 
@@ -366,6 +367,11 @@
     extra = own_0 * inner + own_1 * inner_1 + halo_1 * ghost_1 + halo_2 * ghost_2
 
     outer = (lane < 2) | (lane >= COLS - 2)
+    pieces = [pl.ds(BINS * LEV * n, BINS * LEV) for n in range(BLK * TYPES)]
+    copies = [
+        pltpu.make_async_copy(final.at[rows], out.at[rows], sems.at[n])
+        for n, rows in enumerate(pieces)
+    ]
     for b in range(BLK):
         for t in range(TYPES):
             for l in range(LEV):
@@ -377,19 +383,21 @@
                     final[rows, :] = result[rows, :] + added[8 * q : 8 * q + 8]
                 rows = slice(start + 128, start + 129)
                 final[rows, :] = result[rows, :] + added[32:33]
-        rows = pl.ds(b * (ROWS // BLK), ROWS // BLK)
-        pltpu.make_async_copy(final.at[rows], out.at[rows], sems.at[b]).start()
-    for b in range(BLK):
-        rows = pl.ds(b * (ROWS // BLK), ROWS // BLK)
-        pltpu.make_async_copy(final.at[rows], out.at[rows], sems.at[b]).wait()
+            copies[b * TYPES + t].start()
+    for copy in copies:
+        copy.wait()
 
 
 def vmem(count):
     return [pl.BlockSpec(memory_space=pltpu.VMEM)] * count
 
 
+def placed(space, *arrays):
+    return [pltpu.with_memory_space_constraint(x, space) for x in arrays]
+
+
 def resident(*arrays):
-    return [pltpu.with_memory_space_constraint(x, pltpu.VMEM) for x in arrays]
+    return placed(pltpu.VMEM, *arrays)
 
 
 def body(spectra, collection, growth_rate, fall_speed, supersaturation, courant, cloudy):
@@ -409,11 +417,12 @@
             pltpu.VMEM((KDIM, KDIM), BF16),
             *(pltpu.VMEM(x.shape, x.dtype) for x in sources),
         ),
-        in_specs=[pl.BlockSpec(memory_space=pl.ANY)] * len(sources),
+        in_specs=[pl.BlockSpec(memory_space=pltpu.HBM)] * len(sources),
         out_specs=tuple(vmem(2 + len(sources))),
         scratch_shapes=[pltpu.SemaphoreType.DMA((1 + len(sources),))],
+        compiler_params=pltpu.CompilerParams(vmem_limit_bytes=LIMIT),
         name="edges",
-    )(*sources)
+    )(*placed(pltpu.HBM, *sources))
 
     def blocks(which, edge, held):
         shapes = (
@@ -437,6 +446,7 @@
                 pltpu.VMEM((TYPES * MROWS, KDIM), BF16),
                 pltpu.VMEM((LEV, 40, COLS), F32),
             ],
+            compiler_params=pltpu.CompilerParams(vmem_limit_bytes=LIMIT),
         )(*resident(spec, sat, wind, wet, coll, growth, fall, chosen, edge, *held))
 
     count = lax.axis_size("gy")
@@ -454,8 +464,9 @@
         scratch_shapes=[
             pltpu.VMEM((SUB, 48, COLS), F32),
             pltpu.VMEM((ROWS, COLS), F32),
-            pltpu.SemaphoreType.DMA((BLK,)),
+            pltpu.SemaphoreType.DMA((BLK * TYPES,)),
         ],
+        compiler_params=pltpu.CompilerParams(vmem_limit_bytes=LIMIT),
         name="finish",
     )(*resident(result, rim, from_left, from_right, edge, lhs, coef))
     return out.reshape(spectra.shape)

time: 19.6 us -> 16.5 us (0.84)
  the two profiles are of different devices: /device:TPU:0 before, /device:TPU:54 now
where the time goes in v4:
time: 16.5 us; the launch traced here: 16.4 us
  Pallas kernels  10.5 us (64%)
  waiting for transfers between devices  4.41 us (27%)
  starting transfers between devices  1.41 us (9%)
    pallas_call x2, Pallas kernels, blocks(): pl.pallas_call(lambda *refs: main_kernel(which, *refs), out_shape=shapes,...  7.12 us
    ppermute x1, waiting for transfers between devices, body(): from_left = lax.ppermute(packed, 'gy', up)  2.94 us
    pallas_call x1, Pallas kernels, body(): pl.pallas_call(finish_kernel, out_shape=jax.ShapeDtypeStruct((ROWS, COLS)...  2.04 us
    ppermute x1, waiting for transfers between devices, body(): from_right = lax.ppermute(packed, 'gy', down)  1.47 us
    ppermute x1, starting transfers between devices, body(): from_right = lax.ppermute(packed, 'gy', down)  1.41 us
    pallas_call x1, Pallas kernels, body(): pl.pallas_call(edge_kernel, out_shape=(pltpu.VMEM((40, COLS), F32), pltpu...  1.38 us
  transfers between devices with their start and end apart: 2, of which 2 were waited for; matrix products, arithmetic and copies ran while one was open for 0% of the time, Pallas kernels for 0%

profile of v4, /device:TPU:54, one launch (start us, length us, event | category | flops | bytes accessed | tf_op | source)
XLA Modules:
  0.0 16.4 jit_solution(13768279203953125457)
XLA Ops:
  0.0 1.4 %edges.1 = (f32[40,128]{1,0:T(8,128)S(1)}, bf16[640,640]{1,0:T(8,128)(2,1)S(1)}, f32[1056,128]{1,0:T(8,128)S(1)}, f32[8,128]{1,0:T(8,128)S(1)}, f32[8,128]{1,0:T...) custom-call(f32[1056,128]{1,0:T(8,128)} %bitcast.5, ...), custom_call_target="tpu_custom_call" | custom-call | tf_op jit(solution)/shard_map/edges/pallas_call | solution.py:413
  1.4 7.1 %shard_map.73 = (f32[1056,128]{1,0:T(8,128)S(1)}, f32[40,128]{1,0:T(8,128)S(1)}, bf16[320,640]{1,0:T(8,128)(2,1)S(1)}, f32[8,40,128]{2,1,0:T(8,128)S(1)}, f32[5,...) custom-call(f32[1056,128]{1,0:T(8,128)S(1)} %get-tuple-element.24.refs_0_, f32[8,128]{1,0:T(8,128)S(1)} %get-tuple-element.25.refs_1_, ...), custom_call_target="tpu_custom_call" | custom-call | tf_op jit(solution)/shard_map/pallas_call | solution.py:437
  8.5 1.4 %collective-permute-start.1 = (f32[40,128]{1,0:T(8,128)S(1)}, f32[40,128]{1,0:T(8,128)S(1)}, u32[]{:S(2)}, u32[]{:S(2)}) collective-permute-start(f32[40,128]{1,0:T(8,128)S(1)} %get-tuple-element.33.refs_8_), channel_id=1, source_target_pairs={{1,0},{2,1},{3,2},{4,3},{5,4},{6,5},{7,6},{8,7},{9,8},{10,9},{11,1... | collective-permute-start | bytes 61448 | tf_op jit(solution)/shard_map/ppermute | solution.py:457
  9.9 0.0 collective-permute-start
  9.9 1.5 %collective-permute-done.1.from_right = f32[40,128]{1,0:T(8,128)S(1)} collective-permute-done((f32[40,128]{1,0:T(8,128)S(1)}, f32[40,128]{1,0:T(8,128)S(1)}, u32[]{:S(2)}, u32[]{:S(2)}) %collective-permute-start.1) | collective-permute-done | bytes 20512 | tf_op jit(solution)/shard_map/ppermute | solution.py:457
  11.4 2.9 %collective-permute-done.from_left = f32[40,128]{1,0:T(8,128)S(1)} collective-permute-done((f32[40,128]{1,0:T(8,128)S(1)}, f32[40,128]{1,0:T(8,128)S(1)}, u32[]{:S(2)}, u32[]{:S(2)}) %collective-permute-start) | collective-permute-done | bytes 20512 | tf_op jit(solution)/shard_map/ppermute | solution.py:456
  14.3 2.0 %finish.1 = f32[1056,128]{1,0:T(8,128)} custom-call(f32[1056,128]{1,0:T(8,128)S(1)} %get-tuple-element.39.result, f32[40,128]{1,0:T(8,128)S(1)} %get-tuple-element.40.rim, f32[40,128]{1,0:T(8,128)S(1)} %collective-permute-done.from_left, f32[40,128]{1,0:T(8,128)S(1)} %collective-permute-done.1.from_right, f32[40,128]{1,0:T(8,128)S(1)} %get-tuple-element.32.refs_8_.edge, ...), custom_call_target="tpu_custom_call" | custom-call | tf_op jit(solution)/shard_map/finish/pallas_call | solution.py:459
  (1 shorter events, 0.0 us)
Async XLA Ops:
  8.5 2.9 %collective-permute-start.1 = (f32[40,128]{1,0:T(8,128)S(1)}, f32[40,128]{1,0:T(8,128)S(1)}, u32[]{:S(2)}, u32[]{:S(2)}) collective-permute-start(f32[40,128]{1,0:T(8,128)S(1)} %get-tuple-element.33.refs_8_), channel_id=1, source_target_pairs={{1,0},{2,1},{3,2},{4,3},{5,4},{6,5},{7,6},{8,7},{9,8},{10,9},{11,1... | collective-permute-start | bytes 61448 | tf_op jit(solution)/shard_map/ppermute | solution.py:457
  9.9 4.4 %collective-permute-start = (f32[40,128]{1,0:T(8,128)S(1)}, f32[40,128]{1,0:T(8,128)S(1)}, u32[]{:S(2)}, u32[]{:S(2)}) collective-permute-start(f32[40,128]{1,0:T(8,128)S(1)} %get-tuple-element.33.refs_8_), channel_id=1, source_target_pairs={{0,1},{1,2},{2,3},{3,4},{4,5},{5,6},{6,7},{7,8},{8,9},{9,10},{10,1... | collective-permute-start | bytes 61448 | tf_op jit(solution)/shard_map/ppermute | solution.py:456

commit v5 on v4

--- a/solution.py
+++ b/solution.py
@@ -126,7 +126,7 @@
     for by, value in zip(range(-2, 3), weights(left, right)):
         inside = (lane + by >= 0) & (lane + by < COLS)
         stencil[by + 2] = jnp.where(inside, value, 0.0)
-    raw[...] = jnp.zeros(raw.shape, F32)
+    raw[KDIM // COLS - 1] = jnp.zeros(raw.shape[1:], F32)
     for n in range(KDIM // COLS):
         width = min(COLS, PAIRS - COLS * n)
         for k in range(BINS):
@@ -208,20 +208,32 @@
     return total[:, 0:COLS] + total[:, COLS : 2 * COLS]
 
 
+UP = ((6, 4, 3, 1, 0, 0, 0, 0), (7, 5, 4, 2, 1, 1, 1, 0))
+DOWN = ((8, 5, 4, 2, 1, 1, 1, 0), (7, 5, 4, 2, 1, 1, 1, 0))
+
+
 def shares():
     x, y = lax.axis_index("gx"), lax.axis_index("gy")
-    z = y >> 1
-    first = jnp.int32(0)
-    for n, count in enumerate((8, 7, 5, 3, 1)):
-        first = jnp.where(z == n, count, first)
-    first = jnp.where((x == 0) & (y == 0), 0, first)
-    return (0, first), (first, BLK * TYPES)
+
+    def pick(table):
+        value = jnp.int32(0)
+        for odd in range(2):
+            for z, count in enumerate(table[odd]):
+                value = jnp.where(y == 2 * z + odd, count, value)
+        return value
+
+    origin = (x == 0) & (y == 0)
+    first = jnp.where(origin, 0, pick(UP))
+    second = jnp.where(origin, 1, pick(DOWN))
+    ahead = ((x == 0) & (y == 2)).astype(jnp.int32)
+    first, second = first - ahead, second - ahead
+    return (0, first), (first, second), (second, BLK * TYPES)
 
 
 def main_kernel(which, spec, sat, wind, cloudy, coll, growth, fall, chosen, edge, *rest):
-    result, rim, lhs, coef, stencil = rest[-10:-5] if which == 0 else rest[-9:-4]
+    result, rim, lhs, coef, stencil = rest[-10:-5] if which < 2 else rest[-9:-4]
     turn, raw, parts, held = rest[-4:]
-    if which == 0:
+    if which < 2:
         rest[-5][...] = edge[...]
     begin, end = shares()[which]
     owner = ((iota((1, COLS), 1) + 2) & (COLS - 1)) >> 2
@@ -432,7 +444,7 @@
             pltpu.VMEM((2 * TYPES, 40, COLS), F32),
             pltpu.VMEM((5, BLK * LEV, COLS), F32),
         )
-        if which == 0:
+        if which < 2:
             shapes += (pltpu.VMEM((40, COLS), F32),)
         return pl.pallas_call(
             lambda *refs: main_kernel(which, *refs),
@@ -452,10 +464,11 @@
     count = lax.axis_size("gy")
     up = [(i, (i + 1) % count) for i in range(count)]
     down = [(j, i) for i, j in up]
-    *held, packed = blocks(0, edge, ())
-    from_left = lax.ppermute(packed, "gy", up)
-    from_right = lax.ppermute(packed, "gy", down)
-    result, rim, lhs, coef, _ = blocks(1, packed, held)
+    *held, edge0 = blocks(0, edge, ())
+    from_left = lax.ppermute(edge0, "gy", up)
+    *held, edge1 = blocks(1, edge0, held)
+    from_right = lax.ppermute(edge1, "gy", down)
+    result, rim, lhs, coef, _ = blocks(2, edge1, held)
     out = pl.pallas_call(
         finish_kernel,
         out_shape=jax.ShapeDtypeStruct((ROWS, COLS), F32),

time: 16.5 us -> 16.5 us (level)
  the two profiles are of different devices: /device:TPU:54 before, /device:TPU:60 now
where the time goes in v5:
time: 16.5 us; the launch traced here: 16.4 us
  Pallas kernels  10.8 us (65%)
  waiting for transfers between devices  4.41 us (27%)
  starting transfers between devices  1.23 us (7%)
    pallas_call x3, Pallas kernels, blocks(): pl.pallas_call(lambda *refs: main_kernel(which, *refs), out_shape=shapes,...  7.36 us
    ppermute x1, waiting for transfers between devices, body(): from_left = lax.ppermute(edge0, 'gy', up)  2.94 us
    pallas_call x1, Pallas kernels, body(): pl.pallas_call(finish_kernel, out_shape=jax.ShapeDtypeStruct((ROWS, COLS)...  2.04 us
    ppermute x1, waiting for transfers between devices, body(): from_right = lax.ppermute(edge1, 'gy', down)  1.47 us
    pallas_call x1, Pallas kernels, body(): pl.pallas_call(edge_kernel, out_shape=(pltpu.VMEM((40, COLS), F32), pltpu...  1.38 us
    ppermute x1, starting transfers between devices, body(): from_right = lax.ppermute(edge1, 'gy', down)  1.22 us
  transfers between devices with their start and end apart: 2, of which 2 were waited for; matrix products, arithmetic and copies ran while one was open for 0% of the time, Pallas kernels for 0%

profile of v5, /device:TPU:60, one launch (start us, length us, event | category | flops | bytes accessed | tf_op | source)
XLA Modules:
  0.0 16.4 jit_solution(13015007349806250955)
XLA Ops:
  0.0 1.4 %edges.1 = (f32[40,128]{1,0:T(8,128)S(1)}, bf16[640,640]{1,0:T(8,128)(2,1)S(1)}, f32[1056,128]{1,0:T(8,128)S(1)}, f32[8,128]{1,0:T(8,128)S(1)}, f32[8,128]{1,0:T...) custom-call(f32[1056,128]{1,0:T(8,128)} %bitcast.5, ...), custom_call_target="tpu_custom_call" | custom-call | tf_op jit(solution)/shard_map/edges/pallas_call | solution.py:425
  1.4 5.6 %shard_map.73 = (f32[1056,128]{1,0:T(8,128)S(1)}, f32[40,128]{1,0:T(8,128)S(1)}, bf16[320,640]{1,0:T(8,128)(2,1)S(1)}, f32[8,40,128]{2,1,0:T(8,128)S(1)}, f32[5,...) custom-call(f32[1056,128]{1,0:T(8,128)S(1)} %get-tuple-element.30.refs_0_, f32[8,128]{1,0:T(8,128)S(1)} %get-tuple-element.31.refs_1_, ...), custom_call_target="tpu_custom_call" | custom-call | tf_op jit(solution)/shard_map/pallas_call | solution.py:449
  7.0 1.8 %shard_map.74 = (f32[1056,128]{1,0:T(8,128)S(1)}, f32[40,128]{1,0:T(8,128)S(1)}, bf16[320,640]{1,0:T(8,128)(2,1)S(1)}, f32[8,40,128]{2,1,0:T(8,128)S(1)}, f32[5,...) custom-call(f32[1056,128]{1,0:T(8,128)S(1)} %get-tuple-element.30.re, ...), custom_call_target="tpu_custom_call", output_to_operand_aliasing={{0}: (9, {}), {1}: (10, {}), {2}: (11, {}), {3}: (12, {}), ... | custom-call | tf_op jit(solution)/shard_map/pallas_call | solution.py:449
  8.8 1.2 %collective-permute-start.1 = (f32[40,128]{1,0:T(8,128)S(1)}, f32[40,128]{1,0:T(8,128)S(1)}, u32[]{:S(2)}, u32[]{:S(2)}) collective-permute-start(f32[40,128]{1,0:T(8,128)S(1)} %get-tuple-element.45.refs_8_), channel_id=1, source_target_pairs={{1,0},{2,1},{3,2},{4,3},{5,4},{6,5},{7,6},{8,7},{9,8},{10,9},{11,1... | collective-permute-start | bytes 61448 | tf_op jit(solution)/shard_map/ppermute | solution.py:470
  10.0 0.0 collective-permute-start
  10.0 1.5 %collective-permute-done.1.from_right = f32[40,128]{1,0:T(8,128)S(1)} collective-permute-done((f32[40,128]{1,0:T(8,128)S(1)}, f32[40,128]{1,0:T(8,128)S(1)}, u32[]{:S(2)}, u32[]{:S(2)}) %collective-permute-start.1) | collective-permute-done | bytes 20512 | tf_op jit(solution)/shard_map/ppermute | solution.py:470
  11.5 2.9 %collective-permute-done.from_left = f32[40,128]{1,0:T(8,128)S(1)} collective-permute-done((f32[40,128]{1,0:T(8,128)S(1)}, f32[40,128]{1,0:T(8,128)S(1)}, u32[]{:S(2)}, u32[]{:S(2)}) %collective-permute-start) | collective-permute-done | bytes 20512 | tf_op jit(solution)/shard_map/ppermute | solution.py:468
  14.4 2.0 %finish.1 = f32[1056,128]{1,0:T(8,128)} custom-call(f32[1056,128]{1,0:T(8,128)S(1)} %get-tuple-element.51.result, f32[40,128]{1,0:T(8,128)S(1)} %get-tuple-element.52.rim, f32[40,128]{1,0:T(8,128)S(1)} %collective-permute-done.from_left, f32[40,128]{1,0:T(8,128)S(1)} %collective-permute-done.1.from_right, f32[40,128]{1,0:T(8,128)S(1)} %get-tuple-element.38.refs_8_.edge, ...), custom_call_target="tpu_custom_call" | custom-call | tf_op jit(solution)/shard_map/finish/pallas_call | solution.py:472
  (1 shorter events, 0.0 us)
Async XLA Ops:
  8.8 2.7 %collective-permute-start.1 = (f32[40,128]{1,0:T(8,128)S(1)}, f32[40,128]{1,0:T(8,128)S(1)}, u32[]{:S(2)}, u32[]{:S(2)}) collective-permute-start(f32[40,128]{1,0:T(8,128)S(1)} %get-tuple-element.45.refs_8_), channel_id=1, source_target_pairs={{1,0},{2,1},{3,2},{4,3},{5,4},{6,5},{7,6},{8,7},{9,8},{10,9},{11,1... | collective-permute-start | bytes 61448 | tf_op jit(solution)/shard_map/ppermute | solution.py:470
  10.0 4.4 %collective-permute-start = (f32[40,128]{1,0:T(8,128)S(1)}, f32[40,128]{1,0:T(8,128)S(1)}, u32[]{:S(2)}, u32[]{:S(2)}) collective-permute-start(f32[40,128]{1,0:T(8,128)S(1)} %get-tuple-element.39.refs_8_), channel_id=1, source_target_pairs={{0,1},{1,2},{2,3},{3,4},{4,5},{5,6},{6,7},{7,8},{8,9},{9,10},{10,1... | collective-permute-start | bytes 61448 | tf_op jit(solution)/shard_map/ppermute | solution.py:468

commit v6 on v5

--- a/solution.py
+++ b/solution.py
@@ -208,8 +208,8 @@
     return total[:, 0:COLS] + total[:, COLS : 2 * COLS]
 
 
-UP = ((6, 4, 3, 1, 0, 0, 0, 0), (7, 5, 4, 2, 1, 1, 1, 0))
-DOWN = ((8, 5, 4, 2, 1, 1, 1, 0), (7, 5, 4, 2, 1, 1, 1, 0))
+UP = ((6, 4, 3, 1, 0, 0, 0, 0), (6, 5, 4, 2, 1, 1, 1, 0))
+DOWN = ((7, 5, 4, 2, 1, 1, 1, 0), (6, 5, 4, 2, 1, 1, 1, 0))
 
 
 def shares():
@@ -222,11 +222,11 @@
                 value = jnp.where(y == 2 * z + odd, count, value)
         return value
 
-    origin = (x == 0) & (y == 0)
-    first = jnp.where(origin, 0, pick(UP))
-    second = jnp.where(origin, 1, pick(DOWN))
-    ahead = ((x == 0) & (y == 2)).astype(jnp.int32)
-    first, second = first - ahead, second - ahead
+    first, second = pick(UP), pick(DOWN)
+    for n, pair in enumerate(((0, 1), (6, 6), (1, 2), (4, 5))):
+        special = (x == 0) & (y == n)
+        first = jnp.where(special, pair[0], first)
+        second = jnp.where(special, pair[1], second)
     return (0, first), (first, second), (second, BLK * TYPES)
 
 
@@ -379,7 +379,7 @@
     extra = own_0 * inner + own_1 * inner_1 + halo_1 * ghost_1 + halo_2 * ghost_2
 
     outer = (lane < 2) | (lane >= COLS - 2)
-    pieces = [pl.ds(BINS * LEV * n, BINS * LEV) for n in range(BLK * TYPES)]
+    pieces = [pl.ds(2 * BINS * LEV * n, 2 * BINS * LEV) for n in range(BLK * TYPES // 2)]
     copies = [
         pltpu.make_async_copy(final.at[rows], out.at[rows], sems.at[n])
         for n, rows in enumerate(pieces)
@@ -395,7 +395,8 @@
                     final[rows, :] = result[rows, :] + added[8 * q : 8 * q + 8]
                 rows = slice(start + 128, start + 129)
                 final[rows, :] = result[rows, :] + added[32:33]
-            copies[b * TYPES + t].start()
+            if t & 1:
+                copies[(b * TYPES + t) // 2].start()
     for copy in copies:
         copy.wait()
 
@@ -477,7 +478,7 @@
         scratch_shapes=[
             pltpu.VMEM((SUB, 48, COLS), F32),
             pltpu.VMEM((ROWS, COLS), F32),
-            pltpu.SemaphoreType.DMA((BLK * TYPES,)),
+            pltpu.SemaphoreType.DMA((BLK * TYPES // 2,)),
         ],
         compiler_params=pltpu.CompilerParams(vmem_limit_bytes=LIMIT),
         name="finish",

time: 16.5 us -> 16.5 us (level)
  the two profiles are of different devices: /device:TPU:60 before, /device:TPU:6 now
where the time goes in v6:
time: 16.5 us; the launch traced here: 16.4 us
  Pallas kernels  10.9 us (66%)
  waiting for transfers between devices  3.45 us (21%)
  starting transfers between devices  2 us (12%)
    pallas_call x3, Pallas kernels, blocks(): pl.pallas_call(lambda *refs: main_kernel(which, *refs), out_shape=shapes,...  7.54 us
    ppermute x1, waiting for transfers between devices, body(): from_left = lax.ppermute(edge0, 'gy', up)  2.94 us
    pallas_call x1, Pallas kernels, body(): pl.pallas_call(finish_kernel, out_shape=jax.ShapeDtypeStruct((ROWS, COLS)...  2.01 us
    ppermute x1, starting transfers between devices, body(): from_right = lax.ppermute(edge1, 'gy', down)  2 us
    pallas_call x1, Pallas kernels, body(): pl.pallas_call(edge_kernel, out_shape=(pltpu.VMEM((40, COLS), F32), pltpu...  1.38 us
    ppermute x1, waiting for transfers between devices, body(): from_right = lax.ppermute(edge1, 'gy', down)  0.51 us
  transfers between devices with their start and end apart: 2, of which 2 were waited for; matrix products, arithmetic and copies ran while one was open for 0% of the time, Pallas kernels for 6%

profile of v6, /device:TPU:6, one launch (start us, length us, event | category | flops | bytes accessed | tf_op | source)
XLA Modules:
  0.0 16.4 jit_solution(14223132438420343175)
XLA Ops:
  0.0 1.4 %edges.1 = (f32[40,128]{1,0:T(8,128)S(1)}, bf16[640,640]{1,0:T(8,128)(2,1)S(1)}, f32[1056,128]{1,0:T(8,128)S(1)}, f32[8,128]{1,0:T(8,128)S(1)}, f32[8,128]{1,0:T...) custom-call(f32[1056,128]{1,0:T(8,128)} %bitcast.5, ...), custom_call_target="tpu_custom_call" | custom-call | tf_op jit(solution)/shard_map/edges/pallas_call | solution.py:426
  1.4 5.6 %shard_map.73 = (f32[1056,128]{1,0:T(8,128)S(1)}, f32[40,128]{1,0:T(8,128)S(1)}, bf16[320,640]{1,0:T(8,128)(2,1)S(1)}, f32[8,40,128]{2,1,0:T(8,128)S(1)}, f32[5,...) custom-call(f32[1056,128]{1,0:T(8,128)S(1)} %get-tuple-element.30.refs_0_, f32[8,128]{1,0:T(8,128)S(1)} %get-tuple-element.31.refs_1_, ...), custom_call_target="tpu_custom_call" | custom-call | tf_op jit(solution)/shard_map/pallas_call | solution.py:450
  7.0 1.0 %shard_map.74 = (f32[1056,128]{1,0:T(8,128)S(1)}, f32[40,128]{1,0:T(8,128)S(1)}, bf16[320,640]{1,0:T(8,128)(2,1)S(1)}, f32[8,40,128]{2,1,0:T(8,128)S(1)}, f32[5,...) custom-call(f32[1056,128]{1,0:T(8,128)S(1)} %get-tuple-element.30.re, ...), custom_call_target="tpu_custom_call", output_to_operand_aliasing={{0}: (9, {}), {1}: (10, {}), {2}: (11, {}), {3}: (12, {}), ... | custom-call | tf_op jit(solution)/shard_map/pallas_call | solution.py:450
  8.0 2.0 %collective-permute-start.1 = (f32[40,128]{1,0:T(8,128)S(1)}, f32[40,128]{1,0:T(8,128)S(1)}, u32[]{:S(2)}, u32[]{:S(2)}) collective-permute-start(f32[40,128]{1,0:T(8,128)S(1)} %get-tuple-element.45.refs_8_), channel_id=1, source_target_pairs={{1,0},{2,1},{3,2},{4,3},{5,4},{6,5},{7,6},{8,7},{9,8},{10,9},{11,1... | collective-permute-start | bytes 61448 | tf_op jit(solution)/shard_map/ppermute | solution.py:471
  10.0 0.0 collective-permute-start
  10.0 1.0 %shard_map.75 = (f32[1056,128]{1,0:T(8,128)S(1)}, f32[40,128]{1,0:T(8,128)S(1)}, bf16[320,640]{1,0:T(8,128)(2,1)S(1)}, f32[8,40,128]{2,1,0:T(8,128)S(1)}, f32[5,8,128]{2,1,0:T(8,128)S(1)}) custom-call(f32[1056,128]{1,0:T(8,128)S(1)} %get-tuple-element.30.refs_0_, ...), custom_call_target="tpu_custom_call", output_to_operand_aliasing={{0}: (9, {}), {1}: (10, {}), {2}: (11, {}), {3}: (12, {}), ... | custom-call | tf_op jit(solution)/shard_map/pallas_call | solution.py:450
  11.0 0.5 %collective-permute-done.1.from_right = f32[40,128]{1,0:T(8,128)S(1)} collective-permute-done((f32[40,128]{1,0:T(8,128)S(1)}, f32[40,128]{1,0:T(8,128)S(1)}, u32[]{:S(2)}, u32[]{:S(2)}) %collective-permute-start.1) | collective-permute-done | bytes 20512 | tf_op jit(solution)/shard_map/ppermute | solution.py:471
  11.5 2.9 %collective-permute-done.from_left = f32[40,128]{1,0:T(8,128)S(1)} collective-permute-done((f32[40,128]{1,0:T(8,128)S(1)}, f32[40,128]{1,0:T(8,128)S(1)}, u32[]{:S(2)}, u32[]{:S(2)}) %collective-permute-start) | collective-permute-done | bytes 20512 | tf_op jit(solution)/shard_map/ppermute | solution.py:469
  14.4 2.0 %finish.1 = f32[1056,128]{1,0:T(8,128)} custom-call(f32[1056,128]{1,0:T(8,128)S(1)} %get-tuple-element.51.result, f32[40,128]{1,0:T(8,128)S(1)} %get-tuple-element.52.rim, f32[40,128]{1,0:T(8,128)S(1)} %collective-permute-done.from_left, f32[40,128]{1,0:T(8,128)S(1)} %collective-permute-done.1.from_right, f32[40,128]{1,0:T(8,128)S(1)} %get-tuple-element.38.refs_8_.edge, ...), custom_call_target="tpu_custom_call" | custom-call | tf_op jit(solution)/shard_map/finish/pallas_call | solution.py:473
Async XLA Ops:
  8.0 3.5 %collective-permute-start.1 = (f32[40,128]{1,0:T(8,128)S(1)}, f32[40,128]{1,0:T(8,128)S(1)}, u32[]{:S(2)}, u32[]{:S(2)}) collective-permute-start(f32[40,128]{1,0:T(8,128)S(1)} %get-tuple-element.45.refs_8_), channel_id=1, source_target_pairs={{1,0},{2,1},{3,2},{4,3},{5,4},{6,5},{7,6},{8,7},{9,8},{10,9},{11,1... | collective-permute-start | bytes 61448 | tf_op jit(solution)/shard_map/ppermute | solution.py:471
  10.0 4.4 %collective-permute-start = (f32[40,128]{1,0:T(8,128)S(1)}, f32[40,128]{1,0:T(8,128)S(1)}, u32[]{:S(2)}, u32[]{:S(2)}) collective-permute-start(f32[40,128]{1,0:T(8,128)S(1)} %get-tuple-element.39.refs_8_), channel_id=1, source_target_pairs={{0,1},{1,2},{2,3},{3,4},{4,5},{5,6},{6,7},{7,8},{8,9},{9,10},{10,1... | collective-permute-start | bytes 61448 | tf_op jit(solution)/shard_map/ppermute | solution.py:469

commit v7 on v6

--- a/solution.py
+++ b/solution.py
@@ -379,7 +379,8 @@
     extra = own_0 * inner + own_1 * inner_1 + halo_1 * ghost_1 + halo_2 * ghost_2
 
     outer = (lane < 2) | (lane >= COLS - 2)
-    pieces = [pl.ds(2 * BINS * LEV * n, 2 * BINS * LEV) for n in range(BLK * TYPES // 2)]
+    bounds = [BINS * LEV * n // 8 * 8 for n in range(BLK * TYPES + 1)]
+    pieces = [pl.ds(low, high - low) for low, high in zip(bounds, bounds[1:])]
     copies = [
         pltpu.make_async_copy(final.at[rows], out.at[rows], sems.at[n])
         for n, rows in enumerate(pieces)
@@ -395,8 +396,7 @@
                     final[rows, :] = result[rows, :] + added[8 * q : 8 * q + 8]
                 rows = slice(start + 128, start + 129)
                 final[rows, :] = result[rows, :] + added[32:33]
-            if t & 1:
-                copies[(b * TYPES + t) // 2].start()
+            copies[b * TYPES + t].start()
     for copy in copies:
         copy.wait()
 
@@ -478,7 +478,7 @@
         scratch_shapes=[
             pltpu.VMEM((SUB, 48, COLS), F32),
             pltpu.VMEM((ROWS, COLS), F32),
-            pltpu.SemaphoreType.DMA((BLK * TYPES // 2,)),
+            pltpu.SemaphoreType.DMA((BLK * TYPES,)),
         ],
         compiler_params=pltpu.CompilerParams(vmem_limit_bytes=LIMIT),
         name="finish",

time: 16.5 us -> 16.5 us (level)
  no operation moved by 1% of the time
where the time goes in v7:
time: 16.5 us; the launch traced here: 16.4 us
  Pallas kernels  11 us (67%)
  waiting for transfers between devices  3.45 us (21%)
  starting transfers between devices  2 us (12%)
    pallas_call x3, Pallas kernels, blocks(): pl.pallas_call(lambda *refs: main_kernel(which, *refs), out_shape=shapes,...  7.54 us
    ppermute x1, waiting for transfers between devices, body(): from_left = lax.ppermute(edge0, 'gy', up)  2.94 us
    pallas_call x1, Pallas kernels, body(): pl.pallas_call(finish_kernel, out_shape=jax.ShapeDtypeStruct((ROWS, COLS)...  2.04 us
    ppermute x1, starting transfers between devices, body(): from_right = lax.ppermute(edge1, 'gy', down)  2 us
    pallas_call x1, Pallas kernels, body(): pl.pallas_call(edge_kernel, out_shape=(pltpu.VMEM((40, COLS), F32), pltpu...  1.38 us
    ppermute x1, waiting for transfers between devices, body(): from_right = lax.ppermute(edge1, 'gy', down)  0.51 us
  transfers between devices with their start and end apart: 2, of which 2 were waited for; matrix products, arithmetic and copies ran while one was open for 0% of the time, Pallas kernels for 6%

profile of v7, /device:TPU:6, one launch (start us, length us, event | category | flops | bytes accessed | tf_op | source)
XLA Modules:
  0.0 16.4 jit_solution(693164392270625326)
XLA Ops:
  0.0 1.4 %edges.1 = (f32[40,128]{1,0:T(8,128)S(1)}, bf16[640,640]{1,0:T(8,128)(2,1)S(1)}, f32[1056,128]{1,0:T(8,128)S(1)}, f32[8,128]{1,0:T(8,128)S(1)}, f32[8,128]{1,0:T...) custom-call(f32[1056,128]{1,0:T(8,128)} %bitcast.5, ...), custom_call_target="tpu_custom_call" | custom-call | tf_op jit(solution)/shard_map/edges/pallas_call | solution.py:426
  1.4 5.6 %shard_map.73 = (f32[1056,128]{1,0:T(8,128)S(1)}, f32[40,128]{1,0:T(8,128)S(1)}, bf16[320,640]{1,0:T(8,128)(2,1)S(1)}, f32[8,40,128]{2,1,0:T(8,128)S(1)}, f32[5,...) custom-call(f32[1056,128]{1,0:T(8,128)S(1)} %get-tuple-element.30.refs_0_, f32[8,128]{1,0:T(8,128)S(1)} %get-tuple-element.31.refs_1_, ...), custom_call_target="tpu_custom_call" | custom-call | tf_op jit(solution)/shard_map/pallas_call | solution.py:450
  7.0 1.0 %shard_map.74 = (f32[1056,128]{1,0:T(8,128)S(1)}, f32[40,128]{1,0:T(8,128)S(1)}, bf16[320,640]{1,0:T(8,128)(2,1)S(1)}, f32[8,40,128]{2,1,0:T(8,128)S(1)}, f32[5,...) custom-call(f32[1056,128]{1,0:T(8,128)S(1)} %get-tuple-element.30.re, ...), custom_call_target="tpu_custom_call", output_to_operand_aliasing={{0}: (9, {}), {1}: (10, {}), {2}: (11, {}), {3}: (12, {}), ... | custom-call | tf_op jit(solution)/shard_map/pallas_call | solution.py:450
  8.0 2.0 %collective-permute-start.1 = (f32[40,128]{1,0:T(8,128)S(1)}, f32[40,128]{1,0:T(8,128)S(1)}, u32[]{:S(2)}, u32[]{:S(2)}) collective-permute-start(f32[40,128]{1,0:T(8,128)S(1)} %get-tuple-element.45.refs_8_), channel_id=1, source_target_pairs={{1,0},{2,1},{3,2},{4,3},{5,4},{6,5},{7,6},{8,7},{9,8},{10,9},{11,1... | collective-permute-start | bytes 61448 | tf_op jit(solution)/shard_map/ppermute | solution.py:471
  10.0 0.0 collective-permute-start
  10.0 1.0 %shard_map.75 = (f32[1056,128]{1,0:T(8,128)S(1)}, f32[40,128]{1,0:T(8,128)S(1)}, bf16[320,640]{1,0:T(8,128)(2,1)S(1)}, f32[8,40,128]{2,1,0:T(8,128)S(1)}, f32[5,8,128]{2,1,0:T(8,128)S(1)}) custom-call(f32[1056,128]{1,0:T(8,128)S(1)} %get-tuple-element.30.refs_0_, ...), custom_call_target="tpu_custom_call", output_to_operand_aliasing={{0}: (9, {}), {1}: (10, {}), {2}: (11, {}), {3}: (12, {}), ... | custom-call | tf_op jit(solution)/shard_map/pallas_call | solution.py:450
  11.0 0.5 %collective-permute-done.1.from_right = f32[40,128]{1,0:T(8,128)S(1)} collective-permute-done((f32[40,128]{1,0:T(8,128)S(1)}, f32[40,128]{1,0:T(8,128)S(1)}, u32[]{:S(2)}, u32[]{:S(2)}) %collective-permute-start.1) | collective-permute-done | bytes 20512 | tf_op jit(solution)/shard_map/ppermute | solution.py:471
  11.5 2.9 %collective-permute-done.from_left = f32[40,128]{1,0:T(8,128)S(1)} collective-permute-done((f32[40,128]{1,0:T(8,128)S(1)}, f32[40,128]{1,0:T(8,128)S(1)}, u32[]{:S(2)}, u32[]{:S(2)}) %collective-permute-start) | collective-permute-done | bytes 20512 | tf_op jit(solution)/shard_map/ppermute | solution.py:469
  14.4 2.0 %finish.1 = f32[1056,128]{1,0:T(8,128)} custom-call(f32[1056,128]{1,0:T(8,128)S(1)} %get-tuple-element.51.result, f32[40,128]{1,0:T(8,128)S(1)} %get-tuple-element.52.rim, f32[40,128]{1,0:T(8,128)S(1)} %collective-permute-done.from_left, f32[40,128]{1,0:T(8,128)S(1)} %collective-permute-done.1.from_right, f32[40,128]{1,0:T(8,128)S(1)} %get-tuple-element.38.refs_8_.edge, ...), custom_call_target="tpu_custom_call" | custom-call | tf_op jit(solution)/shard_map/finish/pallas_call | solution.py:473
Async XLA Ops:
  8.0 3.5 %collective-permute-start.1 = (f32[40,128]{1,0:T(8,128)S(1)}, f32[40,128]{1,0:T(8,128)S(1)}, u32[]{:S(2)}, u32[]{:S(2)}) collective-permute-start(f32[40,128]{1,0:T(8,128)S(1)} %get-tuple-element.45.refs_8_), channel_id=1, source_target_pairs={{1,0},{2,1},{3,2},{4,3},{5,4},{6,5},{7,6},{8,7},{9,8},{10,9},{11,1... | collective-permute-start | bytes 61448 | tf_op jit(solution)/shard_map/ppermute | solution.py:471
  10.0 4.4 %collective-permute-start = (f32[40,128]{1,0:T(8,128)S(1)}, f32[40,128]{1,0:T(8,128)S(1)}, u32[]{:S(2)}, u32[]{:S(2)}) collective-permute-start(f32[40,128]{1,0:T(8,128)S(1)} %get-tuple-element.39.refs_8_), channel_id=1, source_target_pairs={{0,1},{1,2},{2,3},{3,4},{4,5},{5,6},{6,7},{7,8},{8,9},{9,10},{10,1... | collective-permute-start | bytes 61448 | tf_op jit(solution)/shard_map/ppermute | solution.py:469

commit v8 on v6

--- a/solution.py
+++ b/solution.py
@@ -52,46 +52,49 @@
 
 def edge_kernel(*refs):
     sources, edge, chosen, kept, sems = refs[:7], refs[7], refs[8], refs[9:16], refs[16]
-    halves = [pl.ds(b * (ROWS // BLK), ROWS // BLK) for b in range(BLK)]
-    pairs = [(sources[0].at[rows], kept[0].at[rows]) for rows in halves]
+    pieces = [pl.ds(2 * BINS * LEV * n, 2 * BINS * LEV) for n in range(BLK * TYPES // 2)]
+    pairs = [(sources[0].at[rows], kept[0].at[rows]) for rows in pieces]
     pairs += list(zip(sources[1:], kept[1:]))
     copies = [pltpu.make_async_copy(*pair, sems.at[n]) for n, pair in enumerate(pairs)]
-    for n in (2, 3, 4, 0, 1, 5, 6, 7):
+    for n in (4, 5, 6, 0, 1, 2, 3, 7, 8, 9):
         copies[n].start()
     wanted = pair_of_column(iota((1, KDIM), 1))
     for first in range(0, KDIM, COLS):
         rows = iota((COLS, KDIM), 0) + first
         chosen[first : first + COLS, :] = jnp.where(rows == wanted, 1.0, 0.0).astype(BF16)
     spec, sat, wind, cloudy = kept[:4]
-    for copy in copies[2:5]:
+    for copy in copies[4:7]:
         copy.wait()
     lane = iota((1, COLS), 1)
     owner = ((lane + 2) & 127) >> 2
     row8 = iota((8, COLS), 0)
     main = [jnp.zeros((8, COLS), F32) for _ in range(4)]
     last = jnp.zeros((8, COLS), F32)
+    extras = [
+        jnp.where(
+            row8 == 1,
+            sat[n : n + 1, :],
+            jnp.where(row8 == 2, wind[n : n + 1, :], cloudy[n // LEV : n // LEV + 1, :].astype(F32)),
+        )
+        for n in range(BLK * LEV)
+    ]
     for b in range(BLK):
-        copies[b].wait()
-        cloud_row = cloudy[b : b + 1, :].astype(F32)
-        for l in range(LEV):
-            extra = jnp.where(
-                row8 == 1,
-                sat[b * LEV + l : b * LEV + l + 1, :],
-                jnp.where(row8 == 2, wind[b * LEV + l : b * LEV + l + 1, :], cloud_row),
-            )
-            for t in range(TYPES):
+        for t in range(TYPES):
+            if t & 1 == 0:
+                copies[(b * TYPES + t) // 2].wait()
+            for l in range(LEV):
                 spot = (t * BLK + b) * LEV + l
                 mine = owner == spot
                 start = block_row(t, b) + l
                 for q in range(4):
                     piece = spec[pl.ds(start + 32 * q, 8, stride=LEV), :]
                     main[q] = jnp.where(mine, pltpu.roll(piece, 4 * spot, 1), main[q])
-                piece = jnp.where(row8 == 0, spec[start + 128 : start + 129, :], extra)
+                piece = jnp.where(row8 == 0, spec[start + 128 : start + 129, :], extras[b * LEV + l])
                 last = jnp.where(mine, pltpu.roll(piece, 4 * spot, 1), last)
     for q in range(4):
         edge[8 * q : 8 * q + 8, :] = main[q]
     edge[32:40, :] = last
-    for copy in copies[5:]:
+    for copy in copies[7:]:
         copy.wait()
 
 
@@ -432,7 +435,7 @@
         ),
         in_specs=[pl.BlockSpec(memory_space=pltpu.HBM)] * len(sources),
         out_specs=tuple(vmem(2 + len(sources))),
-        scratch_shapes=[pltpu.SemaphoreType.DMA((1 + len(sources),))],
+        scratch_shapes=[pltpu.SemaphoreType.DMA((3 + len(sources),))],
         compiler_params=pltpu.CompilerParams(vmem_limit_bytes=LIMIT),
         name="edges",
     )(*placed(pltpu.HBM, *sources))

time: 16.5 us -> 16.6 us (level)
  the two profiles are of different devices: /device:TPU:6 before, /device:TPU:60 now
where the time goes in v8:
time: 16.6 us; the launch traced here: 16.5 us
  Pallas kernels  11 us (66%)
  waiting for transfers between devices  3.45 us (21%)
  starting transfers between devices  2 us (12%)
    pallas_call x3, Pallas kernels, blocks(): pl.pallas_call(lambda *refs: main_kernel(which, *refs), out_shape=shapes,...  7.54 us
    ppermute x1, waiting for transfers between devices, body(): from_left = lax.ppermute(edge0, 'gy', up)  2.94 us
    pallas_call x1, Pallas kernels, body(): pl.pallas_call(finish_kernel, out_shape=jax.ShapeDtypeStruct((ROWS, COLS)...  2.01 us
    ppermute x1, starting transfers between devices, body(): from_right = lax.ppermute(edge1, 'gy', down)  2 us
    pallas_call x1, Pallas kernels, body(): pl.pallas_call(edge_kernel, out_shape=(pltpu.VMEM((40, COLS), F32), pltpu...  1.48 us
    ppermute x1, waiting for transfers between devices, body(): from_right = lax.ppermute(edge1, 'gy', down)  0.51 us
  transfers between devices with their start and end apart: 2, of which 2 were waited for; matrix products, arithmetic and copies ran while one was open for 0% of the time, Pallas kernels for 6%

profile of v8, /device:TPU:60, one launch (start us, length us, event | category | flops | bytes accessed | tf_op | source)
XLA Modules:
  0.0 16.5 jit_solution(12740680441503131749)
XLA Ops:
  0.0 1.5 %edges.1 = (f32[40,128]{1,0:T(8,128)S(1)}, bf16[640,640]{1,0:T(8,128)(2,1)S(1)}, f32[1056,128]{1,0:T(8,128)S(1)}, f32[8,128]{1,0:T(8,128)S(1)}, f32[8,128]{1,0:T...) custom-call(f32[1056,128]{1,0:T(8,128)} %bitcast.5, ...), custom_call_target="tpu_custom_call" | custom-call | tf_op jit(solution)/shard_map/edges/pallas_call | solution.py:429
  1.5 5.6 %shard_map.73 = (f32[1056,128]{1,0:T(8,128)S(1)}, f32[40,128]{1,0:T(8,128)S(1)}, bf16[320,640]{1,0:T(8,128)(2,1)S(1)}, f32[8,40,128]{2,1,0:T(8,128)S(1)}, f32[5,...) custom-call(f32[1056,128]{1,0:T(8,128)S(1)} %get-tuple-element.30.refs_0_, f32[8,128]{1,0:T(8,128)S(1)} %get-tuple-element.31.refs_1_, ...), custom_call_target="tpu_custom_call" | custom-call | tf_op jit(solution)/shard_map/pallas_call | solution.py:453
  7.1 1.0 %shard_map.74 = (f32[1056,128]{1,0:T(8,128)S(1)}, f32[40,128]{1,0:T(8,128)S(1)}, bf16[320,640]{1,0:T(8,128)(2,1)S(1)}, f32[8,40,128]{2,1,0:T(8,128)S(1)}, f32[5,...) custom-call(f32[1056,128]{1,0:T(8,128)S(1)} %get-tuple-element.30.re, ...), custom_call_target="tpu_custom_call", output_to_operand_aliasing={{0}: (9, {}), {1}: (10, {}), {2}: (11, {}), {3}: (12, {}), ... | custom-call | tf_op jit(solution)/shard_map/pallas_call | solution.py:453
  8.1 2.0 %collective-permute-start.1 = (f32[40,128]{1,0:T(8,128)S(1)}, f32[40,128]{1,0:T(8,128)S(1)}, u32[]{:S(2)}, u32[]{:S(2)}) collective-permute-start(f32[40,128]{1,0:T(8,128)S(1)} %get-tuple-element.45.refs_8_), channel_id=1, source_target_pairs={{1,0},{2,1},{3,2},{4,3},{5,4},{6,5},{7,6},{8,7},{9,8},{10,9},{11,1... | collective-permute-start | bytes 61448 | tf_op jit(solution)/shard_map/ppermute | solution.py:474
  10.1 0.0 collective-permute-start
  10.1 1.0 %shard_map.75 = (f32[1056,128]{1,0:T(8,128)S(1)}, f32[40,128]{1,0:T(8,128)S(1)}, bf16[320,640]{1,0:T(8,128)(2,1)S(1)}, f32[8,40,128]{2,1,0:T(8,128)S(1)}, f32[5,8,128]{2,1,0:T(8,128)S(1)}) custom-call(f32[1056,128]{1,0:T(8,128)S(1)} %get-tuple-element.30.refs_0_, ...), custom_call_target="tpu_custom_call", output_to_operand_aliasing={{0}: (9, {}), {1}: (10, {}), {2}: (11, {}), {3}: (12, {}), ... | custom-call | tf_op jit(solution)/shard_map/pallas_call | solution.py:453
  11.1 0.5 %collective-permute-done.1.from_right = f32[40,128]{1,0:T(8,128)S(1)} collective-permute-done((f32[40,128]{1,0:T(8,128)S(1)}, f32[40,128]{1,0:T(8,128)S(1)}, u32[]{:S(2)}, u32[]{:S(2)}) %collective-permute-start.1) | collective-permute-done | bytes 20512 | tf_op jit(solution)/shard_map/ppermute | solution.py:474
  11.6 2.9 %collective-permute-done.from_left = f32[40,128]{1,0:T(8,128)S(1)} collective-permute-done((f32[40,128]{1,0:T(8,128)S(1)}, f32[40,128]{1,0:T(8,128)S(1)}, u32[]{:S(2)}, u32[]{:S(2)}) %collective-permute-start) | collective-permute-done | bytes 20512 | tf_op jit(solution)/shard_map/ppermute | solution.py:472
  14.5 2.0 %finish.1 = f32[1056,128]{1,0:T(8,128)} custom-call(f32[1056,128]{1,0:T(8,128)S(1)} %get-tuple-element.51.result, f32[40,128]{1,0:T(8,128)S(1)} %get-tuple-element.52.rim, f32[40,128]{1,0:T(8,128)S(1)} %collective-permute-done.from_left, f32[40,128]{1,0:T(8,128)S(1)} %collective-permute-done.1.from_right, f32[40,128]{1,0:T(8,128)S(1)} %get-tuple-element.38.refs_8_.edge, ...), custom_call_target="tpu_custom_call" | custom-call | tf_op jit(solution)/shard_map/finish/pallas_call | solution.py:476
Async XLA Ops:
  8.1 3.5 %collective-permute-start.1 = (f32[40,128]{1,0:T(8,128)S(1)}, f32[40,128]{1,0:T(8,128)S(1)}, u32[]{:S(2)}, u32[]{:S(2)}) collective-permute-start(f32[40,128]{1,0:T(8,128)S(1)} %get-tuple-element.45.refs_8_), channel_id=1, source_target_pairs={{1,0},{2,1},{3,2},{4,3},{5,4},{6,5},{7,6},{8,7},{9,8},{10,9},{11,1... | collective-permute-start | bytes 61448 | tf_op jit(solution)/shard_map/ppermute | solution.py:474
  10.1 4.4 %collective-permute-start = (f32[40,128]{1,0:T(8,128)S(1)}, f32[40,128]{1,0:T(8,128)S(1)}, u32[]{:S(2)}, u32[]{:S(2)}) collective-permute-start(f32[40,128]{1,0:T(8,128)S(1)} %get-tuple-element.39.refs_8_), channel_id=1, source_target_pairs={{0,1},{1,2},{2,3},{3,4},{4,5},{5,6},{6,7},{7,8},{8,9},{9,10},{10,1... | collective-permute-start | bytes 61448 | tf_op jit(solution)/shard_map/ppermute | solution.py:472
